TPU v7x, 32 devices: a whole 2x2x4 slice. The times are simulated.
32 devices in a mesh: tensor: 4 (over y, x), context: 2 (over core), dp: 4 (over z).
Axes of the slice: x: 2, y: 2, z: 4, core: 2. Of those that a mesh axis runs over, the one named last changes fastest.
Arguments:
- inputs: bfloat16 [4, 512, 1024], P('dp', 'context'), may hold values from -6 to 6
- norm_gain1: float32 [1024], replicated, may hold values from 0.5 to 1.5
- w_query: bfloat16 [1024, 512], P(None, 'tensor'), may hold values from -0.1875 to 0.1875
- w_key: bfloat16 [1024, 512], P(None, 'tensor'), may hold values from -0.1875 to 0.1875
- w_value: bfloat16 [1024, 1024], P(None, 'tensor'), may hold values from -0.1875 to 0.1875
- w_gate_out: bfloat16 [1024, 1024], P(None, 'tensor'), may hold values from -0.1875 to 0.1875
- w_low_down: bfloat16 [1024, 16], replicated, may hold values from -0.1875 to 0.1875
- w_low_up: bfloat16 [16, 512], P(None, 'tensor'), may hold values from -3 to 3
- forget_bias: float32 [512], P('tensor'), may hold values from -1 to 9, as said below
- head_gain: float32 [256], replicated, may hold values from 0.5 to 1.5
- w_output: bfloat16 [1024, 1024], P('tensor'), may hold values from -0.1875 to 0.1875
- norm_gain2: float32 [1024], replicated, may hold values from 0.5 to 1.5
- w_ffn_gate: bfloat16 [1024, 2816], P(None, 'tensor'), may hold values from -0.1875 to 0.1875
- w_ffn_up: bfloat16 [1024, 2816], P(None, 'tensor'), may hold values from -0.1875 to 0.1875
- w_ffn_down: bfloat16 [2816, 1024], P('tensor'), may hold values from -0.109375 to 0.109375
- cotangent: bfloat16 [4, 512, 1024], P('dp', 'context'), may hold values from -6 to 6
Outputs:
- result: bfloat16 [4, 512, 1024], P('dp', 'context')
- grad_inputs: float32 [4, 512, 1024], P('dp', 'context')
- grad_gain1: float32 [1024], P(('context', 'dp'))
- grad_w_query: float32 [1024, 512], P(('context', 'dp'), 'tensor')
- grad_w_key: float32 [1024, 512], P(('context', 'dp'), 'tensor')
- grad_w_value: float32 [1024, 1024], P(('context', 'dp'), 'tensor')
- grad_w_gate_out: float32 [1024, 1024], P(('context', 'dp'), 'tensor')
- grad_w_low_down: float32 [1024, 16], P(('context', 'dp'))
- grad_w_low_up: float32 [16, 512], P(None, ('tensor', 'context', 'dp'))
- grad_forget_bias: float32 [512], P(('tensor', 'context', 'dp'))
- grad_head_gain: float32 [256], P(('context', 'dp'))
- grad_w_output: float32 [1024, 1024], P('tensor', ('context', 'dp'))
- grad_gain2: float32 [1024], P(('context', 'dp'))
- grad_w_ffn_gate: float32 [1024, 2816], P(('context', 'dp'), 'tensor')
- grad_w_ffn_up: float32 [1024, 2816], P(('context', 'dp'), 'tensor')
- grad_w_ffn_down: float32 [2816, 1024], P('tensor', ('context', 'dp'))
Inputs may be any that keep to these rules, and one draw needn't show every extreme that they name: `forget_bias`: bias of the forget gate's logits, one per key channel.
All inputs are finite; a program needn't handle non-finite values.
Results may differ from a plain program's by a relative error of at most 0.012.
The roundings to bfloat16 on the way count: a program that leaves them out, or rounds other values in their place, can miss the bound.
Values sent between devices are 32-bit elements; how exact they have to be, the bound alone decides.
A program may use at most 128 MiB of HBM per device.

v0:
```python
import jax
import jax.numpy as jnp
from jax import lax
from jax.sharding import PartitionSpec as P

BLOCK = 64


EPS_MODEL = 1e-06
EPS_HEAD = 1e-05
GATE_NORM = 16.0
HIGHEST = lax.Precision.HIGHEST


def carried_in(shard, axis, combine, identity, reverse):
    size, here = (lax.axis_size(axis), lax.axis_index(axis))
    everything = jax.tree.map(lambda part: lax.all_gather(part, axis), shard)
    start = jax.tree.map(
        lambda part, zero: jnp.broadcast_to(jnp.asarray(zero, part.dtype), part.shape),
        shard,
        identity,
    )

    def lap(k, before):
        at = size - 1 - k if reverse else k
        reached = at > here if reverse else at < here
        new = combine(before, jax.tree.map(lambda part: part[at], everything))
        return jax.tree.map(lambda a, b: jnp.where(reached, a, b), new, before)

    return lax.fori_loop(0, size, lap, start)


def block_step(carried, block_in):
    queries, keys_in, values_in, log_rates = block_in
    cumul_log = jnp.cumsum(log_rates, axis=0)
    anchor = 0.5 * cumul_log[-1]
    scores = jnp.dot(
        queries * jnp.exp(cumul_log - anchor),
        (keys_in * jnp.exp(anchor - cumul_log)).T,
        precision=HIGHEST,
    )
    length = queries.shape[0]
    causal = jnp.arange(length)[:, None] >= jnp.arange(length)[None, :]
    scores = jnp.where(causal, scores, 0.0)
    outputs = jnp.dot(scores, values_in, precision=HIGHEST) + jnp.dot(
        queries * jnp.exp(cumul_log), carried, precision=HIGHEST
    )
    end_log = cumul_log[-1]
    updated = jnp.exp(end_log)[:, None] * carried + jnp.dot(
        (keys_in * jnp.exp(end_log - cumul_log)).T, values_in, precision=HIGHEST
    )
    return (updated, outputs)


def gla_core(queries, keys_in, values_in, log_rates, initial):
    block_count = queries.shape[0] // BLOCK
    blocks = (
        queries.reshape(block_count, BLOCK, -1),
        keys_in.reshape(block_count, BLOCK, -1),
        values_in.reshape(block_count, BLOCK, -1),
        log_rates.reshape(block_count, BLOCK, -1),
    )
    final_state, outputs = lax.scan(block_step, initial, blocks)
    return (outputs.reshape(queries.shape[0], -1), final_state)


def rms_scale(rows_in):
    return lax.rsqrt(jnp.mean(rows_in * rows_in, axis=-1, keepdims=True) + EPS_MODEL)


def norm_back(rows_in, scale_rows, gain_in, grad_normed):
    weighted = gain_in * grad_normed
    grad_gain = jnp.sum(grad_normed * rows_in * scale_rows, axis=0)
    grad_rows = scale_rows * (
        weighted
        - rows_in * scale_rows * scale_rows * jnp.mean(weighted * rows_in, axis=-1, keepdims=True)
    )
    return (grad_rows, grad_gain)


def head_gate(outputs, head_gain, gate_in):
    scale_rows = lax.rsqrt(jnp.mean(outputs * outputs, axis=-1, keepdims=True) + EPS_HEAD)
    return outputs * scale_rows * head_gain * jax.nn.silu(gate_in)


def silu_grad(values_in):
    sigmoid_v = jax.nn.sigmoid(values_in)
    return sigmoid_v * (1.0 + values_in * (1.0 - sigmoid_v))


def carry_forward(earlier_pair, later_pair):
    decay_early, state_early = earlier_pair
    decay_late, state_late = later_pair
    return (decay_early * decay_late, decay_late[..., None] * state_early + state_late)


def carry_backward(earlier_pair, later_pair):
    decay_high, grad_high = earlier_pair
    decay_low, grad_low = later_pair
    return (decay_high * decay_low, grad_low + decay_low[..., None] * grad_high)


def shards(
    inputs,
    norm_gain1,
    w_query,
    w_key,
    w_value,
    w_gate_out,
    w_low_down,
    w_low_up,
    forget_bias,
    head_gain,
    w_output,
    norm_gain2,
    w_ffn_gate,
    w_ffn_up,
    w_ffn_down,
    cotangent,
):
    bf16 = jnp.bfloat16
    f32 = jnp.float32
    seqs_here, tok_here, model_width = inputs.shape
    value_dim = head_gain.shape[0]
    heads_here = w_output.shape[0] // value_dim
    key_dim = w_query.shape[1] // heads_here
    key_scale = key_dim ** (-0.5)
    core_all = jax.vmap(jax.vmap(gla_core))

    def to_heads(packed, width_head):
        return packed.reshape(seqs_here, tok_here, heads_here, width_head).transpose(0, 2, 1, 3)

    def from_heads(packed):
        return packed.transpose(0, 2, 1, 3).reshape(seqs_here * tok_here, -1)

    rows_in = inputs.reshape(-1, model_width).astype(f32)
    scale_one = rms_scale(rows_in)
    normed_one = (rows_in * scale_one * norm_gain1).astype(bf16)
    queries = jnp.dot(normed_one, w_query, preferred_element_type=f32) * key_scale
    keys_proj = jnp.dot(normed_one, w_key, preferred_element_type=f32)
    values_proj = jnp.dot(normed_one, w_value, preferred_element_type=f32)
    gate_in = jnp.dot(normed_one, w_gate_out, preferred_element_type=f32)
    low_rank = jnp.dot(normed_one, w_low_down, preferred_element_type=f32)
    logits = jnp.dot(low_rank, w_low_up.astype(f32), precision=HIGHEST) + forget_bias
    log_rates = jax.nn.log_sigmoid(logits) / GATE_NORM
    queries_h = to_heads(queries, key_dim)
    keys_h = to_heads(keys_proj, key_dim)
    values_h = to_heads(values_proj, value_dim)
    rates_h = to_heads(log_rates, key_dim)
    cumul_dev = jnp.cumsum(rates_h, axis=2)
    total_log = cumul_dev[:, :, -1]
    decay_total = jnp.exp(total_log)
    local_state = jnp.einsum(
        "shtk,shtv->shkv",
        keys_h * jnp.exp(total_log[:, :, None] - cumul_dev),
        values_h,
        precision=HIGHEST,
    )
    state_pair = carried_in(
        (decay_total, local_state),
        "context",
        carry_forward,
        (jnp.ones_like(decay_total), jnp.zeros_like(local_state)),
        False,
    )
    state_entry = state_pair[1]
    core_out, core_pull = jax.vjp(core_all, queries_h, keys_h, values_h, rates_h, state_entry)
    outputs = core_out[0].transpose(0, 2, 1, 3).reshape(-1, heads_here, value_dim)
    gate_heads = gate_in.reshape(-1, heads_here, value_dim)
    gated, gate_pull = jax.vjp(head_gate, outputs, head_gain, gate_heads)
    gated_bf = gated.reshape(-1, heads_here * value_dim).astype(bf16)
    attn_sum = lax.psum(jnp.dot(gated_bf, w_output, preferred_element_type=f32), "tensor")
    hidden_res = rows_in + attn_sum
    scale_two = rms_scale(hidden_res)
    normed_two = (hidden_res * scale_two * norm_gain2).astype(bf16)
    ffn_gate = jnp.dot(normed_two, w_ffn_gate, preferred_element_type=f32)
    ffn_up = jnp.dot(normed_two, w_ffn_up, preferred_element_type=f32)
    mixed_act = (jax.nn.silu(ffn_gate) * ffn_up).astype(bf16)
    ffn_sum = lax.psum(jnp.dot(mixed_act, w_ffn_down, preferred_element_type=f32), "tensor")
    result = (hidden_res + ffn_sum).astype(bf16).reshape(inputs.shape)
    grad_out = cotangent.reshape(-1, model_width)
    grad_res = grad_out.astype(f32)
    grad_down = jnp.einsum("rf,rd->fd", mixed_act, grad_out, preferred_element_type=f32)
    grad_mixed = jnp.einsum("rd,fd->rf", grad_out, w_ffn_down, preferred_element_type=f32)
    grad_gate = (grad_mixed * ffn_up * silu_grad(ffn_gate)).astype(bf16)
    grad_up = (grad_mixed * jax.nn.silu(ffn_gate)).astype(bf16)
    grad_ffn_gate = jnp.einsum("rd,rf->df", normed_two, grad_gate, preferred_element_type=f32)
    grad_ffn_up = jnp.einsum("rd,rf->df", normed_two, grad_up, preferred_element_type=f32)
    ffn_part = jnp.einsum(
        "rf,df->rd", grad_gate, w_ffn_gate, preferred_element_type=f32
    ) + jnp.einsum("rf,df->rd", grad_up, w_ffn_up, preferred_element_type=f32)
    grad_normed_two = lax.psum(ffn_part, "tensor")
    grad_two_rows, grad_gain_two = norm_back(hidden_res, scale_two, norm_gain2, grad_normed_two)
    grad_hidden = grad_res + grad_two_rows
    grad_attn = grad_hidden.astype(bf16)
    grad_out_proj = jnp.einsum("rv,rd->vd", gated_bf, grad_attn, preferred_element_type=f32)
    grad_gated = jnp.einsum("rd,vd->rv", grad_attn, w_output, preferred_element_type=f32).reshape(
        -1, heads_here, value_dim
    )
    grad_outputs, grad_gain_head_part, grad_gate_heads = gate_pull(grad_gated)
    grad_outputs_h = grad_outputs.reshape(seqs_here, tok_here, heads_here, value_dim).transpose(
        0, 2, 1, 3
    )
    direct_grad = jnp.einsum(
        "shtk,shtv->shkv", queries_h * jnp.exp(cumul_dev), grad_outputs_h, precision=HIGHEST
    )
    back_pair = carried_in(
        (decay_total, direct_grad),
        "context",
        carry_backward,
        (jnp.ones_like(decay_total), jnp.zeros_like(direct_grad)),
        True,
    )
    grad_q_h, grad_k_h, grad_v_h, grad_lr_h, unused_state = core_pull(
        (grad_outputs_h, back_pair[1])
    )
    grad_logits = from_heads(grad_lr_h) * jax.nn.sigmoid(-logits) / GATE_NORM
    grad_bias = jnp.sum(grad_logits, axis=0)
    grad_low_up = jnp.einsum("rc,rk->ck", low_rank, grad_logits, precision=HIGHEST)
    grad_low = jnp.einsum("rk,ck->rc", grad_logits, w_low_up.astype(f32), precision=HIGHEST)
    grad_low_down_part = jnp.einsum(
        "rd,rc->dc", normed_one.astype(f32), grad_low, precision=HIGHEST
    )
    grad_q = (from_heads(grad_q_h) * key_scale).astype(bf16)
    grad_k = from_heads(grad_k_h).astype(bf16)
    grad_v = from_heads(grad_v_h).astype(bf16)
    grad_g = grad_gate_heads.reshape(-1, heads_here * value_dim).astype(bf16)
    grad_query_w = jnp.einsum("rd,rk->dk", normed_one, grad_q, preferred_element_type=f32)
    grad_key_w = jnp.einsum("rd,rk->dk", normed_one, grad_k, preferred_element_type=f32)
    grad_value_w = jnp.einsum("rd,rv->dv", normed_one, grad_v, preferred_element_type=f32)
    grad_gate_w = jnp.einsum("rd,rv->dv", normed_one, grad_g, preferred_element_type=f32)
    attn_part = (
        jnp.einsum("rk,dk->rd", grad_q, w_query, preferred_element_type=f32)
        + jnp.einsum("rk,dk->rd", grad_k, w_key, preferred_element_type=f32)
        + jnp.einsum("rv,dv->rd", grad_v, w_value, preferred_element_type=f32)
        + jnp.einsum("rv,dv->rd", grad_g, w_gate_out, preferred_element_type=f32)
        + jnp.einsum("rc,dc->rd", grad_low, w_low_down.astype(f32), precision=HIGHEST)
    )
    grad_normed_one, grad_low_down, grad_gain_head = lax.psum(
        (attn_part, grad_low_down_part, grad_gain_head_part), "tensor"
    )
    grad_one_rows, grad_gain_one = norm_back(rows_in, scale_one, norm_gain1, grad_normed_one)
    grad_inputs = (grad_hidden + grad_one_rows).reshape(inputs.shape)
    summed = (
        lax.psum_scatter(grad_gain_one, ("context", "dp"), scatter_dimension=0, tiled=True),
        lax.psum_scatter(grad_query_w, ("context", "dp"), scatter_dimension=0, tiled=True),
        lax.psum_scatter(grad_key_w, ("context", "dp"), scatter_dimension=0, tiled=True),
        lax.psum_scatter(grad_value_w, ("context", "dp"), scatter_dimension=0, tiled=True),
        lax.psum_scatter(grad_gate_w, ("context", "dp"), scatter_dimension=0, tiled=True),
        lax.psum_scatter(grad_low_down, ("context", "dp"), scatter_dimension=0, tiled=True),
        lax.psum_scatter(grad_low_up, ("context", "dp"), scatter_dimension=1, tiled=True),
        lax.psum_scatter(grad_bias, ("context", "dp"), scatter_dimension=0, tiled=True),
        lax.psum_scatter(grad_gain_head, ("context", "dp"), scatter_dimension=0, tiled=True),
        lax.psum_scatter(grad_out_proj, ("context", "dp"), scatter_dimension=1, tiled=True),
        lax.psum_scatter(grad_gain_two, ("context", "dp"), scatter_dimension=0, tiled=True),
        lax.psum_scatter(grad_ffn_gate, ("context", "dp"), scatter_dimension=0, tiled=True),
        lax.psum_scatter(grad_ffn_up, ("context", "dp"), scatter_dimension=0, tiled=True),
        lax.psum_scatter(grad_down, ("context", "dp"), scatter_dimension=1, tiled=True),
    )
    (
        grad_gain1,
        grad_w_query,
        grad_w_key,
        grad_w_value,
        grad_w_gate_out,
        grad_w_low_down,
        grad_w_low_up,
        grad_forget_bias,
        grad_head_gain,
        grad_w_output,
        grad_gain2,
        grad_w_ffn_gate,
        grad_w_ffn_up,
        grad_w_ffn_down,
    ) = summed
    return (
        result,
        grad_inputs,
        grad_gain1,
        grad_w_query,
        grad_w_key,
        grad_w_value,
        grad_w_gate_out,
        grad_w_low_down,
        grad_w_low_up,
        grad_forget_bias,
        grad_head_gain,
        grad_w_output,
        grad_gain2,
        grad_w_ffn_gate,
        grad_w_ffn_up,
        grad_w_ffn_down,
    )


def solution(mesh):
    return jax.shard_map(
        shards,
        mesh=mesh,
        in_specs=(
            P("dp", "context", None),
            P(),
            P(None, "tensor"),
            P(None, "tensor"),
            P(None, "tensor"),
            P(None, "tensor"),
            P(),
            P(None, "tensor"),
            P("tensor"),
            P(),
            P("tensor", None),
            P(),
            P(None, "tensor"),
            P(None, "tensor"),
            P("tensor", None),
            P("dp", "context", None),
        ),
        out_specs=(
            P("dp", "context", None),
            P("dp", "context", None),
            P(("context", "dp")),
            P(("context", "dp"), "tensor"),
            P(("context", "dp"), "tensor"),
            P(("context", "dp"), "tensor"),
            P(("context", "dp"), "tensor"),
            P(("context", "dp"), None),
            P(None, ("tensor", "context", "dp")),
            P(("tensor", "context", "dp")),
            P(("context", "dp")),
            P("tensor", ("context", "dp")),
            P(("context", "dp")),
            P(("context", "dp"), "tensor"),
            P(("context", "dp"), "tensor"),
            P("tensor", ("context", "dp")),
        ),
        check_vma=False,
    )
```

profile of v0, /device:TPU:16, one launch (start us, length us, event | category | flops | bytes accessed | tf_op | source)
XLA Modules:
  0.0 777.2 jit_solution(8419045790289889680)
XLA Ops:
  22.4 28.6 %while.95 = (s32[]{:T(128)}, f32[1,1,128,256]{3,2,1,0:T(8,128)S(1)}, f32[4,1,1,64,256]{4,3,2,1,0:T(8,128)S(1)}, f32[4,1,1,64,128]{4,3,2,1,0:T(8,128)S(1)}, f32[4...) while((s32[]{:T(128)}, ...), condition=%wide.region_7.8_spmd.clone.clone, body=%wide.region_5.7_spmd.clone.sunk.clone | while | flops 69943424 | bytes 1846997 | solution.py:63
  54.8 53.6 %all-reduce.13.cloned.1.call-done = f32[256,1024]{1,0:T(8,128)} async-done(((f32[256,1024]{1,0:T(8,128)}), f32[256,1024]{1,0:T(8,128)}) %all-reduce.13.cloned.1.call-update) | async-done | bytes 1048592 | tf_op jit(solution)/shard_map/psum | solution.py:172
  119.1 2.6 fusion.164
  121.7 48.7 %all-reduce.15.cloned.1.call-done = f32[256,1024]{1,0:T(8,128)} async-done(((f32[256,1024]{1,0:T(8,128)}), f32[256,1024]{1,0:T(8,128)}) %all-reduce.15.cloned.1.call-update) | async-done | bytes 1048592 | tf_op jit(solution)/shard_map/psum | solution.py:192
  179.5 3.3 while.98
  184.2 67.5 %while.96 = (s32[]{:T(128)}, f32[1,1,128,256]{2,3,1,0:T(8,128)S(1)}, f32[4,1,1,64,128]{4,3,2,1,0:T(8,128)}, bf16[4,1,1,64,128]{4,3,2,1,0:T(8,128)(2,1)}, bf16[4,...) while((s32[]{:T(128)}, ...), condition=%wide.region_23.24_spmd.clone.clone, body=%wide.region_17.23_spmd.clone.sunk.clone | while | flops 139329664 | bytes 4669281 | solution.py:63
  268.5 2.5 fusion.125
  272.7 2.4 fusion.149
  275.1 3.1 fusion.117
  279.2 3.2 fusion.170
  282.5 3.1 fusion.169
  290.2 68.1 %all-reduce.17.cloned.1.call-done = (f32[256,1024]{1,0:T(8,128)}, f32[256,1024]{1,0:T(8,128)}) async-done(((f32[256,1024]{1,0:T(8,128)}, f32[256,1024]{1,0:T(8,128)}), (f32[256,1024]{1,0:T(8,128)}, f32[256,1024]{1,0:T(8,128)})) %all-reduce.17.cloned.1.call-update) | async-done | bytes 2097168 | tf_op jit(solution)/shard_map/psum | solution.py:179
  359.8 15.4 %all-reduce.6 = (f32[1024]{0:T(1024)S(1)}, f32[128]{0:T(128)S(1)}, f32[256]{0:T(256)S(1)}, f32[1024]{0:T(1024)S(1)}) all-reduce(f32[1024]{0:T(1024)S(1)} %get-tuple-element.1114, f32[128]{0:T(128)S(1)} %copy-done.56, f32[256]{0:T(256)S(1)} %copy-done.59, ...), channel_id=4, replica_groups=mesh['tensor'=4,'context'=2,'dp'=4] {'context','dp'}, use_global_device_ids=true, to_apply=%region_27.28.clone | all-reduce | flops 2432 | bytes 19456
  377.1 13.6 %reduce-scatter.29.cloned.1.call-done = f32[128,16]{0,1:T(8,128)} async-done(((f32[1024,16]{0,1:T(8,128)}), f32[128,16]{0,1:T(8,128)}) %reduce-scatter.29.cloned.1.call-update) | async-done | bytes 8208 | tf_op jit(solution)/shard_map/reduce_scatter | solution.py:250
  390.6 10.9 %all-reduce.7 = (f32[128,16]{0,1:T(8,128)}, f32[32]{0:T(128)}) all-reduce(f32[128,16]{0,1:T(8,128)} %reduce-scatter.29.cloned.1.call-done, f32[32]{0:T(128)S(1)} %dynamic-slice.5), channel_id=1, replica_groups=mesh['tensor'=4,'context'=2,'dp'=4] {'tensor'}, use_global_device_ids=true, to_apply=%region_32.33 | all-reduce | flops 2080 | bytes 16640 | tf_op jit(solution)/shard_map/psum | solution.py:239
  401.5 3.3 fusion.107
  404.9 20.0 %reduce-scatter.13.cloned.1.call-done = f32[128,128]{1,0:T(8,128)} async-done(((f32[1024,128]{1,0:T(8,128)}), f32[128,128]{1,0:T(8,128)}) %reduce-scatter.13.cloned.1.call-update) | async-done | bytes 65552 | tf_op jit(solution)/shard_map/reduce_scatter | solution.py:246
  424.9 34.4 %reduce-scatter.15.cloned.1.call-done = f32[128,128]{1,0:T(8,128)} async-done(((f32[1024,128]{1,0:T(8,128)}), f32[128,128]{1,0:T(8,128)}) %reduce-scatter.15.cloned.1.call-update) | async-done | bytes 65552 | tf_op jit(solution)/shard_map/reduce_scatter | solution.py:247
  459.3 37.7 %reduce-scatter.21.cloned.1.call-done = f32[256,128]{1,0:T(8,128)} async-done(((f32[256,1024]{1,0:T(8,128)}), f32[256,128]{1,0:T(8,128)}) %reduce-scatter.21.cloned.1.call-update) | async-done | bytes 131088 | tf_op jit(solution)/shard_map/reduce_scatter | solution.py:254
  496.9 37.8 %reduce-scatter.19.cloned.1.call-done = f32[128,256]{1,0:T(8,128)} async-done(((f32[1024,256]{1,0:T(8,128)}), f32[128,256]{1,0:T(8,128)}) %reduce-scatter.19.cloned.1.call-update) | async-done | bytes 131088 | tf_op jit(solution)/shard_map/reduce_scatter | solution.py:249
  534.8 37.8 %reduce-scatter.17.cloned.1.call-done = f32[128,256]{1,0:T(8,128)} async-done(((f32[1024,256]{1,0:T(8,128)}), f32[128,256]{1,0:T(8,128)}) %reduce-scatter.17.cloned.1.call-update) | async-done | bytes 131088 | tf_op jit(solution)/shard_map/reduce_scatter | solution.py:248
  572.6 66.3 %reduce-scatter.27.cloned.1.call-done = f32[704,128]{1,0:T(8,128)} async-done(((f32[704,1024]{1,0:T(8,128)}), f32[704,128]{1,0:T(8,128)}) %reduce-scatter.27.cloned.1.call-update) | async-done | bytes 360464 | tf_op jit(solution)/shard_map/reduce_scatter | solution.py:258
  638.9 65.8 %reduce-scatter.25.cloned.1.call-done = f32[128,704]{0,1:T(8,128)} async-done(((f32[1024,704]{0,1:T(8,128)}), f32[128,704]{0,1:T(8,128)}) %reduce-scatter.25.cloned.1.call-update) | async-done | bytes 360464 | tf_op jit(solution)/shard_map/reduce_scatter | solution.py:257
  704.7 66.0 %reduce-scatter.23.cloned.1.call-done = f32[128,704]{0,1:T(8,128)} async-done(((f32[1024,704]{0,1:T(8,128)}), f32[128,704]{0,1:T(8,128)}) %reduce-scatter.23.cloned.1.call-update) | async-done | bytes 360464 | tf_op jit(solution)/shard_map/reduce_scatter | solution.py:256
  (388 shorter events, 164.1 us)
Async XLA Ops:
  7.2 106.2 %copy-start = (bf16[704,1024]{1,0:T(8,128)(2,1)S(1)}, bf16[704,1024]{1,0:T(8,128)(2,1)}, u32[]{:S(2)}) copy-start(bf16[704,1024]{1,0:T(8,128)(2,1)} %param.38) | copy-start | bytes 4325380
  7.2 101.2 %all-reduce.13.cloned.1.call-start = ((), (), s32[]{:S(2)}) async-start(), calls=%async_computation.10 | async-start | bytes 2097152 | tf_op jit(solution)/shard_map/psum | solution.py:172
  9.9 41.3 %copy-start.2 = (bf16[256,1024]{1,0:T(8,128)(2,1)}, bf16[256,1024]{1,0:T(8,128)(2,1)S(1)}, u32[]{:S(2)}) copy-start(bf16[256,1024]{1,0:T(8,128)(2,1)S(1)} %fusion.102) | copy-start | bytes 1572868
  22.4 28.8 %copy-start.57 = (f32[256]{0:T(256)S(1)}, f32[256]{0:T(256)}, u32[]{:S(2)}) copy-start(f32[256]{0:T(256)} %param.33) | copy-start | bytes 3076
  51.0 125.0 %copy-start.7 = (f32[4,1,1,64,128]{4,3,2,1,0:T(8,128)}, f32[4,1,1,64,128]{4,3,2,1,0:T(8,128)S(1)}, u32[]{:S(2)}) copy-start(f32[4,1,1,64,128]{4,3,2,1,0:T(8,128)S(1)} %get-tuple-element.1931) | copy-start | bytes 393220
  53.4 56.5 %copy-start.40 = (bf16[256,256]{1,0:T(8,128)(2,1)}, bf16[256,256]{1,0:T(8,128)(2,1)S(1)}, u32[]{:S(2)}) copy-start(bf16[256,256]{1,0:T(8,128)(2,1)S(1)} %get-tuple-element.1261) | copy-start | bytes 393220
  53.4 55.0 %copy-start.1 = (bf16[1,256,1024]{2,1,0:T(8,128)(2,1)S(1)}, bf16[1,256,1024]{2,1,0:T(8,128)(2,1)}, u32[]{:S(2)}) copy-start(bf16[1,256,1024]{2,1,0:T(8,128)(2,1)} %param.24) | copy-start | bytes 1572868
  54.8 55.1 %copy-start.50 = (f32[1024]{0:T(1024)S(1)}, f32[1024]{0:T(1024)}, u32[]{:S(2)}) copy-start(f32[1024]{0:T(1024)} %param.35) | copy-start | bytes 12292
  54.8 115.6 %all-reduce.15.cloned.1.call-start = ((), (), s32[]{:S(2)}) async-start(), calls=%async_computation.11 | async-start | bytes 2097152 | tf_op jit(solution)/shard_map/psum | solution.py:192
  117.8 171.0 %reduce-scatter.31.cloned.1.call-start = ((), (), s32[]{:S(2)}) async-start(), calls=%async_computation.21 | async-start | bytes 73728
  201.1 9.5 %copy-start.13 = (f32[4,1,1,64,128]{4,3,2,1,0:T(8,128)}, f32[4,1,1,64,128]{4,3,2,1,0:T(8,128)S(1)}, u32[]{:S(2)}) copy-start(f32[4,1,1,64,128]{4,3,2,1,0:T(8,128)S(1)} %get-tuple-element.1900) | copy-start | bytes 393220 | tf_op jit(solution)/shard_map/transpose(jvp(vmap(vmap())))/while
  234.8 9.5 %copy-start.13 = (f32[4,1,1,64,128]{4,3,2,1,0:T(8,128)}, f32[4,1,1,64,128]{4,3,2,1,0:T(8,128)S(1)}, u32[]{:S(2)}) copy-start(f32[4,1,1,64,128]{4,3,2,1,0:T(8,128)S(1)} %get-tuple-element.1900) | copy-start | bytes 393220 | tf_op jit(solution)/shard_map/transpose(jvp(vmap(vmap())))/while
  255.9 102.4 %all-reduce.17.cloned.1.call-start = ((), (), s32[]{:S(2)}) async-start(), calls=%async_computation.22 | async-start | bytes 4194304 | tf_op jit(solution)/shard_map/psum | solution.py:179
  262.2 128.4 %reduce-scatter.29.cloned.1.call-start = ((), (), s32[]{:S(2)}) async-start(), calls=%async_computation.20 | async-start | bytes 73728 | tf_op jit(solution)/shard_map/reduce_scatter | solution.py:250
  264.9 160.0 %reduce-scatter.13.cloned.1.call-start = ((), (), s32[]{:S(2)}) async-start(), calls=%async_computation.12 | async-start | bytes 589824 | tf_op jit(solution)/shard_map/reduce_scatter | solution.py:246
  267.1 192.2 %reduce-scatter.15.cloned.1.call-start = ((), (), s32[]{:S(2)}) async-start(), calls=%async_computation.13 | async-start | bytes 589824 | tf_op jit(solution)/shard_map/reduce_scatter | solution.py:247
  268.4 228.5 %reduce-scatter.21.cloned.1.call-start = ((), (), s32[]{:S(2)}) async-start(), calls=%async_computation.16 | async-start | bytes 1179648 | tf_op jit(solution)/shard_map/reduce_scatter | solution.py:254
  271.1 263.7 %reduce-scatter.19.cloned.1.call-start = ((), (), s32[]{:S(2)}) async-start(), calls=%async_computation.15 | async-start | bytes 1179648 | tf_op jit(solution)/shard_map/reduce_scatter | solution.py:249
  272.6 299.9 %reduce-scatter.17.cloned.1.call-start = ((), (), s32[]{:S(2)}) async-start(), calls=%async_computation.14 | async-start | bytes 1179648 | tf_op jit(solution)/shard_map/reduce_scatter | solution.py:248
  275.1 363.8 %reduce-scatter.27.cloned.1.call-start = ((), (), s32[]{:S(2)}) async-start(), calls=%async_computation.19 | async-start | bytes 3244032 | tf_op jit(solution)/shard_map/reduce_scatter | solution.py:258
  278.2 426.5 %reduce-scatter.25.cloned.1.call-start = ((), (), s32[]{:S(2)}) async-start(), calls=%async_computation.18 | async-start | bytes 3244032 | tf_op jit(solution)/shard_map/reduce_scatter | solution.py:257
  282.4 488.3 %reduce-scatter.23.cloned.1.call-start = ((), (), s32[]{:S(2)}) async-start(), calls=%async_computation.17 | async-start | bytes 3244032 | tf_op jit(solution)/shard_map/reduce_scatter | solution.py:256
  285.6 74.2 %copy-start.56 = (f32[128]{0:T(128)S(1)}, f32[128]{0:T(128)}, u32[]{:S(2)}) copy-start(f32[128]{0:T(128)} %get-tuple-element.1228) | copy-start | bytes 1540
  285.6 74.2 %copy-start.59 = (f32[256]{0:T(256)S(1)}, f32[256]{0:T(256)}, u32[]{:S(2)}) copy-start(f32[256]{0:T(256)} %get-tuple-element.1116) | copy-start | bytes 3076
  (64 other events, 208.0 us)
Sparse Core Ops, SparseCore 0:
  54.9 53.4 all-reduce.12
  117.9 52.4 all-reduce.14
  256.0 29.6 reduce-scatter.30
  288.7 69.5 all-reduce.16
  361.0 29.6 reduce-scatter.28
  393.3 31.5 reduce-scatter.12
  427.7 31.4 reduce-scatter.14
  462.1 34.7 reduce-scatter.20
  499.8 34.9 reduce-scatter.18
  537.5 35.0 reduce-scatter.16
  575.5 63.3 reduce-scatter.26
  641.6 63.0 reduce-scatter.24
  707.6 63.0 reduce-scatter.22
where the time goes:
time: 784 us; the launch traced here: 777 us
  waiting for transfers between devices  550 us (70%)
  matrix products  104 us (13%)
  other arithmetic  37.8 us (5%)
  local copies, waits for them, and re-layouts  35.3 us (5%)
  blocking collectives  32.2 us (4%)
  between operations  16.7 us (2%)
    psum x1, waiting for transfers between devices, shards(): lax.psum(jnp.dot(mixed_act, w_ffn_down, preferred_element_type=f32), 'ten...  68.1 us
    reduce_scatter x1, waiting for transfers between devices, shards(): lax.psum_scatter(grad_down, ('context', 'dp'), scatter_dimension=1, tiled...  66.3 us
    reduce_scatter x1, waiting for transfers between devices, shards(): lax.psum_scatter(grad_ffn_gate, ('context', 'dp'), scatter_dimension=0, t...  66 us
    reduce_scatter x1, waiting for transfers between devices, shards(): lax.psum_scatter(grad_ffn_up, ('context', 'dp'), scatter_dimension=0, til...  65.8 us
    psum x1, waiting for transfers between devices, shards(): lax.psum(jnp.dot(gated_bf, w_output, preferred_element_type=f32), 'tensor')  53.6 us
    psum x1, waiting for transfers between devices, shards(): grad_normed_two = lax.psum(ffn_part, 'tensor')  48.7 us
    reduce_scatter x1, waiting for transfers between devices, shards(): lax.psum_scatter(grad_gate_w, ('context', 'dp'), scatter_dimension=0, til...  37.8 us
    reduce_scatter x1, waiting for transfers between devices, shards(): lax.psum_scatter(grad_value_w, ('context', 'dp'), scatter_dimension=0, ti...  37.8 us
  transfers between devices with their start and end apart: 13, of which 12 were waited for; matrix products, arithmetic and copies ran while one was open for 5% of the time, Pallas kernels for 0%

commit v1 on v0

v1 whole, which is shorter than its diff:
```python
import functools

import jax
import jax.numpy as jnp
from jax import lax
from jax.experimental import pallas as pl
from jax.experimental.pallas import tpu as pltpu
from jax.sharding import PartitionSpec as P

BLOCK = 64


EPS_MODEL = 1e-06
EPS_HEAD = 1e-05
GATE_NORM = 16.0
HIGHEST = lax.Precision.HIGHEST


VMEM_LIMIT = 60 * 1024 * 1024
VMEM = pltpu.MemorySpace.VMEM
MESH_ID = pl.DeviceIdType.MESH


def hdot(left, right, dims):
    return lax.dot_general(
        left, right, (dims, ((), ())), precision=HIGHEST, preferred_element_type=jnp.float32
    )


def column_of(row, height):
    return jnp.broadcast_to(row, (height, row.shape[1])).T


def triangle(length):
    rows = lax.broadcasted_iota(jnp.int32, (length, length), 0)
    cols = lax.broadcasted_iota(jnp.int32, (length, length), 1)
    return rows >= cols


def gla_forward_kernel(q_ref, k_ref, v_ref, r_ref, out_ref, decayed_ref, states_ref, pair_ref):
    tokens, key_dim = q_ref.shape
    value_dim = v_ref.shape[1]
    causal = triangle(BLOCK)
    ones_low = causal.astype(jnp.float32)
    state = jnp.zeros((key_dim, value_dim), jnp.float32)
    before = jnp.zeros((1, key_dim), jnp.float32)
    for block in range(tokens // BLOCK):
        span = pl.ds(block * BLOCK, BLOCK)
        queries, keys_in, values_in = q_ref[span, :], k_ref[span, :], v_ref[span, :]
        cumul = hdot(ones_low, r_ref[span, :], ((1,), (0,)))
        end_log = cumul[BLOCK - 1 :, :]
        anchor = 0.5 * end_log
        scores = hdot(
            queries * jnp.exp(cumul - anchor), keys_in * jnp.exp(anchor - cumul), ((1,), (1,))
        )
        scores = jnp.where(causal, scores, 0.0)
        out_ref[span, :] = hdot(scores, values_in, ((1,), (0,))) + hdot(
            queries * jnp.exp(cumul), state, ((1,), (0,))
        )
        decayed_ref[span, :] = queries * jnp.exp(cumul + before)
        states_ref[block] = state
        added = hdot(keys_in * jnp.exp(end_log - cumul), values_in, ((0,), (0,)))
        state = column_of(jnp.exp(end_log), key_dim)[:, :1] * state + added
        before = before + end_log
    pair_ref[:, :value_dim] = state
    pair_ref[:, value_dim:] = column_of(jnp.exp(before), key_dim)


def gla_forward(queries, keys_in, values_in, log_rates):
    tokens, key_dim = queries.shape
    value_dim = values_in.shape[1]
    f32 = jnp.float32
    return pl.pallas_call(
        gla_forward_kernel,
        out_shape=(
            jax.ShapeDtypeStruct((tokens, value_dim), f32),
            jax.ShapeDtypeStruct((tokens, key_dim), f32),
            jax.ShapeDtypeStruct((tokens // BLOCK, key_dim, value_dim), f32),
            jax.ShapeDtypeStruct((key_dim, value_dim + key_dim), f32),
        ),
        compiler_params=pltpu.CompilerParams(vmem_limit_bytes=VMEM_LIMIT),
        name="gla_forward",
    )(queries, keys_in, values_in, log_rates)


def gla_backward_kernel(
    q_ref, k_ref, v_ref, r_ref, states_ref, entry_ref, later_ref, g_ref, dq_ref, dk_ref, dv_ref, dr_ref
):
    tokens, key_dim = q_ref.shape
    causal = triangle(BLOCK)
    ones_low = causal.astype(jnp.float32)
    blocks = tokens // BLOCK
    cumuls, befores = [], []
    before = jnp.zeros((1, key_dim), jnp.float32)
    for block in range(blocks):
        cumul = hdot(ones_low, r_ref[pl.ds(block * BLOCK, BLOCK), :], ((1,), (0,)))
        cumuls.append(cumul)
        befores.append(before)
        before = before + cumul[BLOCK - 1 :, :]
    grad_state = later_ref[...]
    entry = entry_ref[...]
    for block in reversed(range(blocks)):
        span = pl.ds(block * BLOCK, BLOCK)
        queries, keys_in, values_in = q_ref[span, :], k_ref[span, :], v_ref[span, :]
        grad_out = g_ref[span, :]
        cumul = cumuls[block]
        end_log = cumul[BLOCK - 1 :, :]
        anchor = 0.5 * end_log
        state = states_ref[block] + column_of(jnp.exp(befores[block]), key_dim)[:, :1] * entry
        up, down = jnp.exp(cumul - anchor), jnp.exp(anchor - cumul)
        grow, rest = jnp.exp(cumul), jnp.exp(end_log - cumul)
        q_up, k_down = queries * up, keys_in * down
        scores = jnp.where(causal, hdot(q_up, k_down, ((1,), (1,))), 0.0)
        grad_scores = jnp.where(causal, hdot(grad_out, values_in, ((1,), (1,))), 0.0)
        grad_q = hdot(grad_scores, k_down, ((1,), (0,))) * up + grow * hdot(
            grad_out, state, ((1,), (1,))
        )
        carried_k = hdot(values_in, grad_state, ((1,), (1,))) * rest
        grad_k = hdot(grad_scores, q_up, ((0,), (0,))) * down + carried_k
        dv_ref[span, :] = hdot(scores, grad_out, ((0,), (0,))) + hdot(
            keys_in * rest, grad_state, ((1,), (0,))
        )
        dq_ref[span, :] = grad_q
        dk_ref[span, :] = grad_k
        grad_cumul = queries * grad_q - keys_in * grad_k
        end_column = column_of(jnp.exp(end_log), key_dim)
        state_term = jnp.sum(grad_state * state, axis=1, keepdims=True) * end_column
        grad_end = state_term.T[:1, :] + jnp.sum(carried_k * keys_in, axis=0, keepdims=True)
        dr_ref[span, :] = hdot(ones_low, grad_cumul, ((0,), (0,))) + grad_end
        grad_state = end_column[:, :1] * grad_state + hdot(
            queries * grow, grad_out, ((0,), (0,))
        )


def gla_backward(queries, keys_in, values_in, log_rates, states, entry, later, grad_out):
    shaped = tuple(
        jax.ShapeDtypeStruct(part.shape, jnp.float32)
        for part in (queries, keys_in, values_in, log_rates)
    )
    return pl.pallas_call(
        gla_backward_kernel,
        out_shape=shaped,
        compiler_params=pltpu.CompilerParams(vmem_limit_bytes=VMEM_LIMIT),
        name="gla_backward",
    )(queries, keys_in, values_in, log_rates, states, entry, later, grad_out)


def exchange_kernel(size, reverse, value_dim, pair_ref, out_ref, slots, send_sem, recv_sem):
    here = lax.axis_index("context")
    barrier = pltpu.get_barrier_semaphore()
    for step in range(1, size):
        peer = lax.rem(here + step, size)
        pl.semaphore_signal(barrier, inc=1, device_id={"context": peer}, device_id_type=MESH_ID)
    pl.semaphore_wait(barrier, size - 1)
    copies = []
    for step in range(1, size):
        peer = lax.rem(here + step, size)
        copies.append(
            pltpu.make_async_remote_copy(
                src_ref=pair_ref,
                dst_ref=slots.at[step - 1],
                send_sem=send_sem.at[step - 1],
                recv_sem=recv_sem.at[step - 1],
                device_id={"context": peer},
                device_id_type=MESH_ID,
            )
        )
    for copy in copies:
        copy.start()
    for copy in copies:
        copy.wait()
    out_ref[...] = jnp.zeros_like(out_ref)
    order = range(1, size) if reverse else reversed(range(1, size))
    if reverse:
        for m in reversed(range(1, size)):

            @pl.when(here + m < size)
            def _(m=m):
                part = slots.at[size - m - 1]
                out_ref[...] = part[:, value_dim : value_dim + 1] * out_ref[...] + part[:, :value_dim]
    else:
        for step in order:

            @pl.when(here >= step)
            def _(step=step):
                part = slots.at[step - 1]
                out_ref[...] = part[:, value_dim : value_dim + 1] * out_ref[...] + part[:, :value_dim]


def exchange(pair, value_dim, reverse, collective_id):
    size = lax.axis_size("context")
    return pl.pallas_call(
        functools.partial(exchange_kernel, size, reverse, value_dim),
        out_shape=jax.ShapeDtypeStruct((pair.shape[0], value_dim), jnp.float32),
        in_specs=[pl.BlockSpec(memory_space=VMEM)],
        out_specs=pl.BlockSpec(memory_space=VMEM),
        scratch_shapes=[
            pltpu.VMEM((size - 1,) + pair.shape, jnp.float32),
            pltpu.SemaphoreType.DMA((size - 1,)),
            pltpu.SemaphoreType.DMA((size - 1,)),
        ],
        compiler_params=pltpu.CompilerParams(
            collective_id=collective_id, has_side_effects=True, vmem_limit_bytes=VMEM_LIMIT
        ),
        name="exchange_back" if reverse else "exchange",
    )(pair)


def sums_kernel(sizes, n_all, pieces, tail, *refs):
    n_ctx, n_dp, n_ten = sizes
    n_sc = len(pieces)
    take = iter(refs)
    all_in = [next(take) for _ in range(n_all)]
    sc_in = [next(take) for _ in range(n_sc)]
    all_out = [next(take) for _ in range(n_all)]
    sc_out = [next(take) for _ in range(n_sc)]
    all_slots = [next(take) for _ in range(n_all)]
    all_sems = [next(take) for _ in range(n_all)]
    near = [next(take) for _ in range(n_sc)]
    near_sems = [next(take) for _ in range(n_sc)]
    line = [next(take) for _ in range(n_sc)]
    line_sems = [next(take) for _ in range(n_sc)]
    if tail:
        tail_slots, tail_sems = next(take), next(take)
    ctx = lax.axis_index("context")
    dp = lax.axis_index("dp")
    ten = lax.axis_index("tensor")
    use_ten = n_all > 0 or tail

    def peers(index, size):
        return [lax.rem(index + step, size) for step in range(1, size)]

    def remote(src, dst, sems, at, axis, peer):
        return pltpu.make_async_remote_copy(
            src_ref=src,
            dst_ref=dst,
            send_sem=sems.at[(0,) + at],
            recv_sem=sems.at[(1,) + at],
            device_id={axis: peer},
            device_id_type=MESH_ID,
        )

    barrier = pltpu.get_barrier_semaphore()

    def greet(axis, peer):
        pl.semaphore_signal(barrier, inc=1, device_id={axis: peer}, device_id_type=MESH_ID)

    expect = 0
    if n_sc:
        for peer in peers(ctx, n_ctx):
            greet("context", peer)
        expect += n_ctx - 1
    if use_ten:
        for peer in peers(ten, n_ten):
            greet("tensor", peer)
        expect += n_ten - 1
    if n_sc:

        @pl.when(dp > 0)
        def _():
            greet("dp", dp - 1)

        @pl.when(dp < n_dp - 1)
        def _():
            greet("dp", dp + 1)

    if n_sc:
        inner = jnp.logical_and(dp > 0, dp < n_dp - 1)

        @pl.when(inner)
        def _():
            pl.semaphore_wait(barrier, expect + 2)

        @pl.when(jnp.logical_not(inner))
        def _():
            pl.semaphore_wait(barrier, expect + 1)

    else:
        pl.semaphore_wait(barrier, expect)

    def rows(i, piece):
        height = sc_in[i].shape[1] // pieces[i]
        return pl.ds(piece * height, height)

    def near_copy(i, step, dest, piece):
        peer = lax.rem(ctx + step, n_ctx)
        return remote(
            sc_in[i].at[peer * n_dp + dest, rows(i, piece)],
            near[i].at[step - 1, dest, rows(i, piece)],
            near_sems[i],
            (step - 1, dest, piece),
            "context",
            peer,
        )

    def line_copy(i, way, dest, piece, peer):
        place = line[i].at[way, dest, rows(i, piece)]
        return remote(place, place, line_sems[i], (way, dest, piece), "dp", peer)

    def all_copy(i, step):
        peer = lax.rem(ten + step, n_ten)
        return remote(
            all_in[i].at[peer], all_slots[i].at[step - 1], all_sems[i], (0, step - 1), "tensor", peer
        )

    def all_share(i, step):
        peer = lax.rem(ten + step, n_ten)
        return remote(
            all_out[i].at[ten], all_out[i].at[ten], all_sems[i], (1, step - 1), "tensor", peer
        )

    def over_pieces(i, body):
        if pieces[i] == 1:
            body(0)
        else:

            def lap(piece, carry):
                body(piece)
                return carry

            lax.fori_loop(0, pieces[i], lap, 0)

    order = []
    for k in range(n_dp):
        for dest in (n_dp - 1 - k, k):
            if dest not in order:
                order.append(dest)
    for i in range(n_all):
        for step in range(1, n_ten):
            all_copy(i, step).start()
    for dest in order:
        for i in range(n_sc):
            for step in range(1, n_ctx):
                over_pieces(i, lambda piece: near_copy(i, step, dest, piece).start())

    def own_sum(i, dest, piece):
        total = sc_in[i][ctx * n_dp + dest, rows(i, piece)]
        for step in range(1, n_ctx):
            near_copy(i, step, dest, piece).wait_recv()
            total = total + near[i][step - 1, dest, rows(i, piece)]
        return total

    def pass_on(i, way, dest, piece):
        forward = way == 0
        active = dp < dest if forward else dp > dest
        first = dp == (0 if forward else n_dp - 1)
        peer = dp + 1 if forward else dp - 1
        back = dp - 1 if forward else dp + 1

        @pl.when(active)
        def _():
            own = own_sum(i, dest, piece)

            @pl.when(first)
            def _():
                line[i][way, dest, rows(i, piece)] = own

            @pl.when(jnp.logical_not(first))
            def _():
                line_copy(i, way, dest, piece, back).wait_recv()
                line[i][way, dest, rows(i, piece)] = line[i][way, dest, rows(i, piece)] + own

            line_copy(i, way, dest, piece, peer).start()

    def reduce_all():
        for i in range(n_all):
            total = all_in[i][ten]
            for step in range(1, n_ten):
                all_copy(i, step).wait_recv()
                total = total + all_slots[i][step - 1]
            all_out[i][ten] = total
            for step in range(1, n_ten):
                all_share(i, step).start()

    if not n_sc:
        reduce_all()
    else:
        for k in range(n_dp - 1):

            def both(piece, i, k=k):
                pass_on(i, 0, n_dp - 1 - k, piece)
                pass_on(i, 1, k, piece)

            for i in range(n_sc):
                over_pieces(i, functools.partial(both, i=i))
            if k == 0:
                reduce_all()

    for i in range(n_sc):

        def finish(piece, i=i):
            sc_out[i][rows(i, piece), :] = own_sum(i, dp, piece)

            @pl.when(dp > 0)
            def _():
                line_copy(i, 0, dp, piece, dp - 1).wait_recv()
                sc_out[i][rows(i, piece), :] += line[i][0, dp, rows(i, piece)]

            @pl.when(dp < n_dp - 1)
            def _():
                line_copy(i, 1, dp, piece, dp + 1).wait_recv()
                sc_out[i][rows(i, piece), :] += line[i][1, dp, rows(i, piece)]

        over_pieces(i, finish)

    if tail:
        last = sc_out[n_sc - 1]
        tail_slots[ten] = last[:tail, :]

        def tail_copy(step):
            peer = lax.rem(ten + step, n_ten)
            return remote(
                tail_slots.at[ten], tail_slots.at[ten], tail_sems, (step - 1,), "tensor", peer
            )

        def tail_come(step):
            sender = lax.rem(ten + n_ten - step, n_ten)
            return remote(
                tail_slots.at[sender], tail_slots.at[sender], tail_sems, (step - 1,), "tensor", sender
            )

        for step in range(1, n_ten):
            tail_copy(step).start()
        for step in range(1, n_ten):
            tail_come(step).wait_recv()
        total = tail_slots[0]
        for index in range(1, n_ten):
            total = total + tail_slots[index]
        last[:tail, :] = total
        for step in range(1, n_ten):
            tail_copy(step).wait_send()

    for i in range(n_all):
        for step in range(1, n_ten):
            all_copy(i, step).wait_send()
            sender = lax.rem(ten + n_ten - step, n_ten)
            remote(
                all_out[i].at[sender],
                all_out[i].at[sender],
                all_sems[i],
                (1, step - 1),
                "tensor",
                sender,
            ).wait_recv()
            all_share(i, step).wait_send()
    for i in range(n_sc):
        for dest in range(n_dp):

            def drain(piece, i=i, dest=dest):
                for step in range(1, n_ctx):
                    near_copy(i, step, dest, piece).wait_send()

                @pl.when(dp < dest)
                def _():
                    line_copy(i, 0, dest, piece, dp + 1).wait_send()

                @pl.when(dp > dest)
                def _():
                    line_copy(i, 1, dest, piece, dp - 1).wait_send()

            over_pieces(i, drain)


def summed_arrays(whole, scattered, tail, collective_id, name):
    n_ctx, n_dp, n_ten = (lax.axis_size(axis) for axis in ("context", "dp", "tensor"))
    owners = n_ctx * n_dp
    f32 = jnp.float32
    whole_in = [part.reshape(n_ten, part.shape[0] // n_ten, part.shape[1]) for part in whole]
    sc_in = [part.reshape(owners, part.shape[0] // owners, part.shape[1]) for part in scattered]
    pieces = []
    for part in sc_in:
        count = 4
        while part.shape[1] % (count * 8):
            count //= 2
        pieces.append(count if part.shape[2] > 128 else 1)
    scratch = [pltpu.VMEM((n_ten - 1,) + part.shape[1:], f32) for part in whole_in]
    scratch += [pltpu.SemaphoreType.DMA((2, 2, n_ten - 1)) for _ in whole_in]
    scratch += [pltpu.VMEM((n_ctx - 1, n_dp) + part.shape[1:], f32) for part in sc_in]
    scratch += [pltpu.SemaphoreType.DMA((2, n_ctx - 1, n_dp, count)) for count in pieces]
    scratch += [pltpu.VMEM((2, n_dp) + part.shape[1:], f32) for part in sc_in]
    scratch += [pltpu.SemaphoreType.DMA((2, 2, n_dp, count)) for count in pieces]
    if tail:
        scratch += [
            pltpu.VMEM((n_ten, tail, scattered[-1].shape[1]), f32),
            pltpu.SemaphoreType.DMA((2, n_ten - 1)),
        ]
    outs = pl.pallas_call(
        functools.partial(sums_kernel, (n_ctx, n_dp, n_ten), len(whole), tuple(pieces), tail),
        out_shape=tuple(
            [jax.ShapeDtypeStruct(part.shape, f32) for part in whole_in]
            + [jax.ShapeDtypeStruct(part.shape[1:], f32) for part in sc_in]
        ),
        in_specs=[pl.BlockSpec(memory_space=VMEM)] * (len(whole) + len(scattered)),
        out_specs=tuple([pl.BlockSpec(memory_space=VMEM)] * (len(whole) + len(scattered))),
        scratch_shapes=scratch,
        compiler_params=pltpu.CompilerParams(
            collective_id=collective_id, has_side_effects=True, vmem_limit_bytes=VMEM_LIMIT
        ),
        name=name,
    )(*whole_in, *sc_in)
    totals = [out.reshape(part.shape) for out, part in zip(outs, whole)]
    return totals, list(outs[len(whole) :])


def rms_scale(rows_in):
    return lax.rsqrt(jnp.mean(rows_in * rows_in, axis=-1, keepdims=True) + EPS_MODEL)


def norm_back(rows_in, scale_rows, gain_in, grad_normed):
    weighted = gain_in * grad_normed
    grad_gain = jnp.sum(grad_normed * rows_in * scale_rows, axis=0)
    grad_rows = scale_rows * (
        weighted
        - rows_in * scale_rows * scale_rows * jnp.mean(weighted * rows_in, axis=-1, keepdims=True)
    )
    return (grad_rows, grad_gain)


def head_gate(outputs, head_gain, gate_in):
    scale_rows = lax.rsqrt(jnp.mean(outputs * outputs, axis=-1, keepdims=True) + EPS_HEAD)
    return outputs * scale_rows * head_gain * jax.nn.silu(gate_in)


def silu_grad(values_in):
    sigmoid_v = jax.nn.sigmoid(values_in)
    return sigmoid_v * (1.0 + values_in * (1.0 - sigmoid_v))


def shards(
    inputs,
    norm_gain1,
    w_query,
    w_key,
    w_value,
    w_gate_out,
    w_low_down,
    w_low_up,
    forget_bias,
    head_gain,
    w_output,
    norm_gain2,
    w_ffn_gate,
    w_ffn_up,
    w_ffn_down,
    cotangent,
):
    bf16 = jnp.bfloat16
    f32 = jnp.float32
    seqs_here, tok_here, model_width = inputs.shape
    value_dim = head_gain.shape[0]
    heads_here = w_output.shape[0] // value_dim
    key_dim = w_query.shape[1] // heads_here
    key_scale = key_dim ** (-0.5)
    rows_in = inputs.reshape(-1, model_width).astype(f32)
    scale_one = rms_scale(rows_in)
    normed_one = (rows_in * scale_one * norm_gain1).astype(bf16)
    queries = jnp.dot(normed_one, w_query, preferred_element_type=f32) * key_scale
    keys_proj = jnp.dot(normed_one, w_key, preferred_element_type=f32)
    values_proj = jnp.dot(normed_one, w_value, preferred_element_type=f32)
    gate_in = jnp.dot(normed_one, w_gate_out, preferred_element_type=f32)
    low_rank = jnp.dot(normed_one, w_low_down, preferred_element_type=f32)
    logits = jnp.dot(low_rank, w_low_up.astype(f32), precision=HIGHEST) + forget_bias
    log_rates = jax.nn.log_sigmoid(logits) / GATE_NORM
    pairs = [(s, h) for s in range(seqs_here) for h in range(heads_here)]

    def one(packed, s, h, width):
        return packed[s * tok_here : (s + 1) * tok_here, h * width : (h + 1) * width]

    def join(parts):
        return jnp.concatenate(
            [
                jnp.concatenate(parts[s * heads_here : (s + 1) * heads_here], axis=1)
                for s in range(seqs_here)
            ],
            axis=0,
        )

    def stacked(parts):
        return jnp.concatenate(parts, axis=0)

    cores = [
        gla_forward(
            one(queries, s, h, key_dim),
            one(keys_proj, s, h, key_dim),
            one(values_proj, s, h, value_dim),
            one(log_rates, s, h, key_dim),
        )
        for s, h in pairs
    ]
    pair_all = stacked([core[3] for core in cores])
    entry_all = exchange(pair_all, value_dim, False, 0)
    entries = [entry_all[i * key_dim : (i + 1) * key_dim] for i in range(len(pairs))]
    outputs = join(
        [
            core[0] + jnp.dot(core[1], entry, precision=HIGHEST)
            for core, entry in zip(cores, entries)
        ]
    ).reshape(-1, heads_here, value_dim)
    gate_heads = gate_in.reshape(-1, heads_here, value_dim)
    gated, gate_pull = jax.vjp(head_gate, outputs, head_gain, gate_heads)
    gated_bf = gated.reshape(-1, heads_here * value_dim).astype(bf16)
    attn_part_out = jnp.dot(gated_bf, w_output, preferred_element_type=f32)
    (attn_sum,), _ = summed_arrays([attn_part_out], [], 0, 1, "sum_attn")
    hidden_res = rows_in + attn_sum
    scale_two = rms_scale(hidden_res)
    normed_two = (hidden_res * scale_two * norm_gain2).astype(bf16)
    ffn_gate = jnp.dot(normed_two, w_ffn_gate, preferred_element_type=f32)
    ffn_up = jnp.dot(normed_two, w_ffn_up, preferred_element_type=f32)
    mixed_act = (jax.nn.silu(ffn_gate) * ffn_up).astype(bf16)
    ffn_down_part = jnp.dot(mixed_act, w_ffn_down, preferred_element_type=f32)
    grad_out = cotangent.reshape(-1, model_width)
    grad_res = grad_out.astype(f32)
    grad_down_t = jnp.einsum("rd,rf->df", grad_out, mixed_act, preferred_element_type=f32)
    grad_mixed = jnp.einsum("rd,fd->rf", grad_out, w_ffn_down, preferred_element_type=f32)
    grad_gate = (grad_mixed * ffn_up * silu_grad(ffn_gate)).astype(bf16)
    grad_up = (grad_mixed * jax.nn.silu(ffn_gate)).astype(bf16)
    grad_pair = jnp.concatenate([grad_gate, grad_up], axis=1)
    grad_pair_w = jnp.einsum("rd,rf->df", normed_two, grad_pair, preferred_element_type=f32)
    ffn_part = jnp.einsum(
        "rf,df->rd", grad_gate, w_ffn_gate, preferred_element_type=f32
    ) + jnp.einsum("rf,df->rd", grad_up, w_ffn_up, preferred_element_type=f32)
    (grad_normed_two, ffn_sum), (pair_rows, down_rows) = summed_arrays(
        [ffn_part, ffn_down_part], [grad_pair_w, grad_down_t], 0, 2, "sum_ffn"
    )
    result = (hidden_res + ffn_sum).astype(bf16).reshape(inputs.shape)
    grad_two_rows, grad_gain_two = norm_back(hidden_res, scale_two, norm_gain2, grad_normed_two)
    grad_hidden = grad_res + grad_two_rows
    grad_attn = grad_hidden.astype(bf16)
    grad_out_t = jnp.einsum("rd,rv->dv", grad_attn, gated_bf, preferred_element_type=f32)
    grad_gated = jnp.einsum("rd,vd->rv", grad_attn, w_output, preferred_element_type=f32).reshape(
        -1, heads_here, value_dim
    )
    grad_outputs, grad_gain_head_part, grad_gate_heads = gate_pull(grad_gated)
    grad_outputs = grad_outputs.reshape(-1, heads_here * value_dim)
    back_pair = stacked(
        [
            jnp.concatenate(
                [
                    jnp.einsum(
                        "tk,tv->kv", core[1], one(grad_outputs, s, h, value_dim), precision=HIGHEST
                    ),
                    core[3][:, value_dim:],
                ],
                axis=1,
            )
            for core, (s, h) in zip(cores, pairs)
        ]
    )
    later_all = exchange(back_pair, value_dim, True, 3)
    pulled = [
        gla_backward(
            one(queries, s, h, key_dim),
            one(keys_proj, s, h, key_dim),
            one(values_proj, s, h, value_dim),
            one(log_rates, s, h, key_dim),
            cores[i][2],
            entries[i],
            later_all[i * key_dim : (i + 1) * key_dim],
            one(grad_outputs, s, h, value_dim),
        )
        for i, (s, h) in enumerate(pairs)
    ]
    grad_q_all, grad_k_all, grad_v_all, grad_lr_all = (
        join([pull[j] for pull in pulled]) for j in range(4)
    )
    grad_logits = grad_lr_all * jax.nn.sigmoid(-logits) / GATE_NORM
    grad_bias = jnp.sum(grad_logits, axis=0)
    grad_low_up = jnp.einsum("rc,rk->ck", low_rank, grad_logits, precision=HIGHEST)
    grad_low = jnp.einsum("rk,ck->rc", grad_logits, w_low_up.astype(f32), precision=HIGHEST)
    grad_low_down_part = jnp.einsum(
        "rd,rc->dc", normed_one.astype(f32), grad_low, precision=HIGHEST
    )
    grad_q = (grad_q_all * key_scale).astype(bf16)
    grad_k = grad_k_all.astype(bf16)
    grad_v = grad_v_all.astype(bf16)
    grad_g = grad_gate_heads.reshape(-1, heads_here * value_dim).astype(bf16)
    grad_proj = jnp.concatenate([grad_q, grad_k, grad_v, grad_g], axis=1)
    grad_proj_w = jnp.einsum("rd,rk->dk", normed_one, grad_proj, preferred_element_type=f32)
    attn_part = (
        jnp.einsum("rk,dk->rd", grad_q, w_query, preferred_element_type=f32)
        + jnp.einsum("rk,dk->rd", grad_k, w_key, preferred_element_type=f32)
        + jnp.einsum("rv,dv->rd", grad_v, w_value, preferred_element_type=f32)
        + jnp.einsum("rv,dv->rd", grad_g, w_gate_out, preferred_element_type=f32)
        + jnp.einsum("rc,dc->rd", grad_low, w_low_down.astype(f32), precision=HIGHEST)
    )
    gain_one_part = jnp.sum(attn_part * rows_in * scale_one, axis=0)
    owners = lax.axis_size("context") * lax.axis_size("dp")

    def packed_rows(parts):
        flat = jnp.concatenate(parts, axis=1)
        padded = -(-flat.shape[1] // 1024) * 1024
        flat = jnp.pad(flat, ((0, 0), (0, padded - flat.shape[1])))
        return flat.reshape(owners, -1, 128)

    rank = low_rank.shape[1]
    width_up = w_low_up.shape[1]
    tensor_pack = packed_rows(
        [
            grad_low_down_part.reshape(owners, -1),
            gain_one_part.reshape(owners, -1),
            grad_gain_head_part.reshape(owners, -1),
        ]
    )
    local_pack = packed_rows(
        [
            grad_gain_two.reshape(owners, -1),
            grad_low_up.reshape(rank, owners, -1).transpose(1, 0, 2).reshape(owners, -1),
            grad_bias.reshape(owners, -1),
        ]
    )
    pack = jnp.concatenate([tensor_pack, local_pack], axis=1)
    tail = tensor_pack.shape[1]
    (grad_normed_one,), (proj_rows, out_rows, pack_rows) = summed_arrays(
        [attn_part], [grad_proj_w, grad_out_t, pack.reshape(-1, 128)], tail, 4, "sum_attn_back"
    )
    grad_one_rows, _ = norm_back(rows_in, scale_one, norm_gain1, grad_normed_one)
    grad_inputs = (grad_hidden + grad_one_rows).reshape(inputs.shape)
    flat_ten, flat_own = pack_rows[:tail].reshape(-1), pack_rows[tail:].reshape(-1)
    part_model = model_width // owners
    part_head = value_dim // owners
    part_up = width_up // owners
    grad_w_low_down = flat_ten[: part_model * rank].reshape(part_model, rank)
    grad_gain1 = flat_ten[part_model * rank : part_model * (rank + 1)]
    grad_head_gain = flat_ten[part_model * (rank + 1) : part_model * (rank + 1) + part_head]
    grad_gain2 = flat_own[:part_model]
    grad_w_low_up = flat_own[part_model : part_model + rank * part_up].reshape(rank, part_up)
    grad_forget_bias = flat_own[part_model + rank * part_up : part_model + (rank + 1) * part_up]
    width_q = heads_here * key_dim
    width_v = heads_here * value_dim
    grad_w_query = proj_rows[:, :width_q]
    grad_w_key = proj_rows[:, width_q : 2 * width_q]
    grad_w_value = proj_rows[:, 2 * width_q : 2 * width_q + width_v]
    grad_w_gate_out = proj_rows[:, 2 * width_q + width_v :]
    grad_w_output = out_rows.T
    width_ffn = w_ffn_gate.shape[1]
    grad_w_ffn_gate = pair_rows[:, :width_ffn]
    grad_w_ffn_up = pair_rows[:, width_ffn:]
    grad_w_ffn_down = down_rows.T
    return (
        result,
        grad_inputs,
        grad_gain1,
        grad_w_query,
        grad_w_key,
        grad_w_value,
        grad_w_gate_out,
        grad_w_low_down,
        grad_w_low_up,
        grad_forget_bias,
        grad_head_gain,
        grad_w_output,
        grad_gain2,
        grad_w_ffn_gate,
        grad_w_ffn_up,
        grad_w_ffn_down,
    )


def solution(mesh):
    return jax.shard_map(
        shards,
        mesh=mesh,
        in_specs=(
            P("dp", "context", None),
            P(),
            P(None, "tensor"),
            P(None, "tensor"),
            P(None, "tensor"),
            P(None, "tensor"),
            P(),
            P(None, "tensor"),
            P("tensor"),
            P(),
            P("tensor", None),
            P(),
            P(None, "tensor"),
            P(None, "tensor"),
            P("tensor", None),
            P("dp", "context", None),
        ),
        out_specs=(
            P("dp", "context", None),
            P("dp", "context", None),
            P(("context", "dp")),
            P(("context", "dp"), "tensor"),
            P(("context", "dp"), "tensor"),
            P(("context", "dp"), "tensor"),
            P(("context", "dp"), "tensor"),
            P(("context", "dp"), None),
            P(None, ("tensor", "context", "dp")),
            P(("tensor", "context", "dp")),
            P(("context", "dp")),
            P("tensor", ("context", "dp")),
            P(("context", "dp")),
            P(("context", "dp"), "tensor"),
            P(("context", "dp"), "tensor"),
            P("tensor", ("context", "dp")),
        ),
        check_vma=False,
    )
```

time: 784 us -> 346 us (0.44)
  waiting for transfers between devices: 550 us -> 0 us
  Pallas kernels: 0 us -> 235 us
  matrix products: 104 us -> 39.6 us
  blocking collectives: 32.2 us -> 0 us
  between operations: 16.7 us -> 1.31 us
  other arithmetic: 37.8 us -> 23.4 us
  local copies, waits for them, and re-layouts: 35.3 us -> 44.7 us
    reduce_scatter x9 -> x0, waiting for transfers between devices: 379 us -> none  [the longest x1 66.3 us: shards(): lax.psum_scatter(grad_down, ('context', 'dp'), scatter_dimension=1, tiled...]
    pallas_call x0 -> x7, Pallas kernels: none -> 235 us  [the longest x3 219 us: summed_arrays(): pl.pallas_call(functools.partial(sums_kernel, (n_ctx, n_dp, n_ten), len(w...]
    psum x3 -> x0, waiting for transfers between devices: 170 us -> none  [the longest x1 68.1 us: shards(): lax.psum(jnp.dot(mixed_act, w_ffn_down, preferred_element_type=f32), 'ten...]
    dot_general x60 -> x9, matrix products: 83.5 us -> 18.2 us  [the longest x1 4.75 us: shards(): jnp.einsum('rd,rf->df', normed_two, grad_pair, preferred_element_type=f32)]
    unnamed x1 -> x0, blocking collectives: 15.4 us -> none
    psum x1 -> x0, blocking collectives: 10.9 us -> none  [shards(): lax.psum((attn_part, grad_low_down_part, grad_gain_head_part), 'tensor')]
    slice x0 -> x9, local copies, waits for them, and re-layouts: none -> 9.84 us  [the longest x1 1.68 us: shards(): grad_w_gate_out = proj_rows[:, 2 * width_q + width_v:]]
    dot_general x0 -> x4, local copies, waits for them, and re-layouts: none -> 9.7 us  [the longest x1 3.57 us: shards(): jnp.einsum('rd,rf->df', grad_out, mixed_act, preferred_element_type=f32)]
  transfers between devices with their start and end apart: 13 -> 0, of which waited for: 12 -> 0; matrix products, arithmetic and copies ran while one was open for 5% -> 0% of each run, Pallas kernels for 0% -> 0%
where the time goes in v1:
time: 346 us; the launch traced here: 344 us
  Pallas kernels  235 us (68%)
  local copies, waits for them, and re-layouts  44.7 us (13%)
  matrix products  39.6 us (11%)
  other arithmetic  23.4 us (7%)
    pallas_call x3, Pallas kernels, summed_arrays(): pl.pallas_call(functools.partial(sums_kernel, (n_ctx, n_dp, n_ten), len(w...  219 us
    unnamed x121, local copies, waits for them, and re-layouts  12.4 us

profile of v1, /device:TPU:16, one launch (start us, length us, event | category | flops | bytes accessed | tf_op | source)
XLA Modules:
  0.0 344.5 jit_solution(9389365655730351672)
XLA Ops:
  9.1 4.1 %gla_forward.1 = (f32[256,256]{1,0:T(8,128)}, f32[256,128]{1,0:T(8,128)}, f32[4,128,256]{2,1,0:T(8,128)}, f32[128,384]{1,0:T(8,128)}) custom-call(f32[256,128]{1,0:T(8,128)} %convolution_multiply_fusion.q_ref, f32[256,128]{1,0:T(8,128)} %fusion.58.k_ref, f32[256,256]{1,0:T(8,128)} %fusion.56.v_ref, f32[256,128]{1,0:T(8,128)} %get-tuple-element.104.r_ref), custom_call_target="tpu_custom_call" | custom-call | tf_op jit(solution)/shard_map/gla_forward/pallas_call | solution.py:73
  14.7 3.0 exchange.1.entry_ref
  21.7 31.0 %sum_attn.1 = f32[4,64,1024]{2,1,0:T(8,128)} custom-call(f32[4,64,1024]{2,1,0:T(8,128)} %fusion.26.refs_0_), custom_call_target="tpu_custom_call" | custom-call | tf_op jit(solution)/shard_map/sum_attn/pallas_call | solution.py:487
  52.7 2.4 multiply_reduce_fusion.3
  56.2 2.0 copy.62
  58.3 2.2 fusion.65
  65.7 2.1 convolution_bitcast_fusion
  67.8 3.6 %copy.47 = f32[1024,704]{1,0:T(8,128)} copy(f32[1024,704]{0,1:T(8,128)} %convolution_bitcast_fusion) | data formatting | bytes 5767168 | tf_op jit(solution)/shard_map/rd,rf->df/dot_general | solution.py:613
  71.4 4.8 %fusion.19.refs_2_ = f32[8,128,1408]{2,1,0:T(8,128)} fusion(bf16[8,128,256]{2,1,0:T(8,128)(2,1)} %bitcast.191, bf16[256,704]{0,1:T(8,128)(2,1)} %copy-done.12, bf16[256,704]{0,1:T(8,128)(2,1)} %copy-done.11), kind=kOutput, calls=%fused_computation.44 | convolution fusion | flops 739639296 | bytes 7012352 | tf_op jit(solution)/shard_map/rd,rf->df/dot_general | solution.py:618
  76.2 105.3 %sum_ffn.1 = (f32[4,64,1024]{2,1,0:T(8,128)}, f32[4,64,1024]{2,1,0:T(8,128)}, f32[128,1408]{1,0:T(8,128)}, f32[128,704]{1,0:T(8,128)}) custom-call(f32[4,64,1024]{2,1,0:T(8,128)} %bitcast.188, f32[4,64,1024]{2,1,0:T(8,128)} %bitcast.187, f32[8,128,1408]{2,1,0:T(8,128)} %fusion.19.refs_2_, f32[8,128,704]{2,1,0:T(8,128)} %bitcast.182), custom_call_target="tpu_custom_call" | custom-call | tf_op jit(solution)/shard_map/sum_ffn/pallas_call | solution.py:487
  181.5 2.4 multiply_reduce_fusion.1
  185.3 1.9 copy.58
  191.6 3.1 exchange_back.1.later_ref
  194.8 5.9 %gla_backward.1 = (f32[256,128]{1,0:T(8,128)}, f32[256,128]{1,0:T(8,128)}, f32[256,256]{1,0:T(8,128)}, f32[256,128]{1,0:T(8,128)}) custom-call(f32[256,128]{1,0:T(8,128)} %convolution_multiply_fusion.q_ref, f32[256,128]{1,0:T(8,128)} %fusion.58.k_ref, f32[256,256]{1,0:T(8,128)} %fusion.56.v_ref, f32[256,128]{1,0:T(8,128)} %get-tuple-element.104.r_ref, ...), custom_call_target="tpu_custom_call" | custom-call | tf_op jit(solution)/shard_map/gla_backward/pallas_call | solution.py:140
  215.1 2.3 fusion.49
  217.3 1.9 reshape.393
  219.3 2.0 copy.65
  221.3 2.4 fusion.41.refs_2_
  224.7 1.9 copy.57
  226.6 1.9 copy.56
  236.3 2.0 copy.64
  238.4 3.3 fusion.28.refs_1_
  241.7 83.0 %sum_attn_back.1 = (f32[4,64,1024]{2,1,0:T(8,128)}, f32[128,768]{1,0:T(8,128)}, f32[128,256]{1,0:T(8,128)}, f32[32,128]{1,0:T(8,128)}) custom-call(f32[4,64,1024]{2,1,0:T(8,128)} %bitcast.183, f32[8,128,768]{2,1,0:T(8,128)} %fusion.28.refs_1_, f32[8,128,256]{2,1,0:T(8,128)} %fusion.41.refs_2_, f32[8,32,128]{2,1,0:T(8,128)} %pad_maximum_fusion.1.refs_3_), custom_call_target="tpu_custom_call" | custom-call | tf_op jit(solution)/shard_map/sum_attn_back/pallas_call | solution.py:487
  332.3 3.7 %fusion.2 = (f32[1,256,1024]{2,1,0:T(8,128)}, bf16[1,256,1024]{2,1,0:T(8,128)(2,1)}) fusion(bf16[1,256,1024]{2,1,0:T(8,128)(2,1)S(1)} %copy-done.1, bf16[1,256,1024]{2,1,0:T(8,128)(2,1)S(1)} %copy-done.4, f32[256]{0:T(256)} %div.62, f32[1024]{0:T(1024)S(1)} %copy-done.38, f32[256]{0:T(256)S(1)} %copy-done.44, f32[256]{0:T(256)} %copy-done.50, ...), kind=kLoop, calls=%fused_computation.12 | loop fusion | flops 4980736 | bytes 6828032 | tf_op jit(solution)/shard_map/add | solution.py:717
  (180 shorter events, 64.7 us)
Async XLA Ops:
  0.6 59.8 %copy-start = (bf16[1024,704]{0,1:T(8,128)(2,1)S(1)}, bf16[1024,704]{0,1:T(8,128)(2,1)}, u32[]{:S(2)}) copy-start(bf16[1024,704]{0,1:T(8,128)(2,1)} %param.29) | copy-start | bytes 4325380
  0.7 2.8 copy-start.1
  0.7 2.8 copy-start.36
  0.7 2.8 copy-start.28
  0.7 3.9 %copy-start.33 = (bf16[1024,128]{1,0:T(8,128)(2,1)S(1)}, bf16[1024,128]{1,0:T(8,128)(2,1)}, u32[]{:S(2)}) copy-start(bf16[1024,128]{1,0:T(8,128)(2,1)} %param.18) | copy-start | bytes 786436
  2.1 17.2 %copy-start.42 = (f32[256]{0:T(256)}, f32[256]{0:T(256)S(1)}, u32[]{:S(2)}) copy-start(f32[256]{0:T(256)S(1)} %add_rsqrt_fusion.1) | copy-start | bytes 3076
  3.5 3.2 copy-start.45
  4.6 3.1 copy-start.4
  4.6 3.1 copy-start.5
  9.1 10.2 %copy-start.23 = (bf16[1024,256]{1,0:T(8,128)(2,1)S(1)}, bf16[1024,256]{1,0:T(8,128)(2,1)}, u32[]{:S(2)}) copy-start(bf16[1024,256]{1,0:T(8,128)(2,1)} %param.21) | copy-start | bytes 1572868
  9.1 10.2 %copy-start.54 = (f32[256]{0:T(256)S(1)}, f32[256]{0:T(256)}, u32[]{:S(2)}) copy-start(f32[256]{0:T(256)} %param.25) | copy-start | bytes 3076
  52.7 2.5 copy-start.2
  52.7 2.5 copy-start.39
  55.2 131.9 %copy-start.48 = (f32[256]{0:T(256)}, f32[256]{0:T(256)S(1)}, u32[]{:S(2)}) copy-start(f32[256]{0:T(256)S(1)} %rsqrt.34) | copy-start | bytes 3076
  61.3 2.8 copy-start.11
  61.3 2.8 copy-start.12
  185.3 3.7 %copy-start.50 = (f32[256]{0:T(256)}, f32[256]{0:T(256)S(1)}, u32[]{:S(2)}) copy-start(f32[256]{0:T(256)S(1)} %div.56) | copy-start | bytes 3076
  190.2 4.5 %copy-start.9 = (f32[256,256]{1,0:T(8,128)}, f32[256,256]{1,0:T(8,128)S(1)}, u32[]{:S(2)}) copy-start(f32[256,256]{1,0:T(8,128)S(1)} %add_add_fusion.g_ref) | copy-start | bytes 786436
  190.3 10.4 %copy-start.34 = (f32[256,128]{1,0:T(8,128)S(1)}, f32[256,128]{1,0:T(8,128)}, u32[]{:S(2)}) copy-start(f32[256,128]{1,0:T(8,128)} %get-tuple-element.105) | copy-start | bytes 393220
  190.9 12.0 %copy-start.46 = (f32[256,16]{0,1:T(8,128)S(1)}, f32[256,16]{0,1:T(8,128)}, u32[]{:S(2)}) copy-start(f32[256,16]{0,1:T(8,128)} %copy-done.45) | copy-start | bytes 49156
  241.7 87.2 %copy-start.38 = (f32[1024]{0:T(1024)S(1)}, f32[1024]{0:T(1024)}, u32[]{:S(2)}) copy-start(f32[1024]{0:T(1024)} %param.17) | copy-start | bytes 12292
  324.8 7.5 %copy-start.40 = (f32[1024]{0:T(1024)S(1)}, f32[1024]{0:T(1024)}, u32[]{:S(2)}) copy-start(f32[1024]{0:T(1024)} %param.27) | copy-start | bytes 12292
  324.8 7.5 %copy-start.44 = (f32[256]{0:T(256)S(1)}, f32[256]{0:T(256)}, u32[]{:S(2)}) copy-start(f32[256]{0:T(256)} %copy-done.42) | copy-start | bytes 3076
  324.8 7.5 %copy-start.49 = (f32[256]{0:T(256)S(1)}, f32[256]{0:T(256)}, u32[]{:S(2)}) copy-start(f32[256]{0:T(256)} %copy-done.48) | copy-start | bytes 3076
  (33 other events, 51.3 us)

commit v2 on v1

--- a/solution.py
+++ b/solution.py
@@ -206,12 +206,12 @@
     )(pair)
 
 
-def sums_kernel(sizes, n_all, pieces, tail, *refs):
+def sums_kernel(sizes, n_all, pieces, made, tail, *refs):
     n_ctx, n_dp, n_ten = sizes
     n_sc = len(pieces)
     take = iter(refs)
     all_in = [next(take) for _ in range(n_all)]
-    sc_in = [next(take) for _ in range(n_sc)]
+    factors = [(next(take), next(take) if is_made else None) for is_made in made]
     all_out = [next(take) for _ in range(n_all)]
     sc_out = [next(take) for _ in range(n_sc)]
     all_slots = [next(take) for _ in range(n_all)]
@@ -220,6 +220,7 @@
     near_sems = [next(take) for _ in range(n_sc)]
     line = [next(take) for _ in range(n_sc)]
     line_sems = [next(take) for _ in range(n_sc)]
+    sc_in = [next(take) if right is not None else left for left, right in factors]
     if tail:
         tail_slots, tail_sems = next(take), next(take)
     ctx = lax.axis_index("context")
@@ -328,10 +329,19 @@
     for i in range(n_all):
         for step in range(1, n_ten):
             all_copy(i, step).start()
+    def make(i, owner):
+        left, right = factors[i]
+        if right is not None:
+            sc_in[i][owner] = jnp.dot(
+                left[owner], right[...], preferred_element_type=jnp.float32
+            )
+
     for dest in order:
         for i in range(n_sc):
             for step in range(1, n_ctx):
+                make(i, lax.rem(ctx + step, n_ctx) * n_dp + dest)
                 over_pieces(i, lambda piece: near_copy(i, step, dest, piece).start())
+            make(i, ctx * n_dp + dest)
 
     def own_sum(i, dest, piece):
         total = sc_in[i][ctx * n_dp + dest, rows(i, piece)]
@@ -466,7 +476,14 @@
     owners = n_ctx * n_dp
     f32 = jnp.float32
     whole_in = [part.reshape(n_ten, part.shape[0] // n_ten, part.shape[1]) for part in whole]
-    sc_in = [part.reshape(owners, part.shape[0] // owners, part.shape[1]) for part in scattered]
+    made = tuple(isinstance(part, tuple) for part in scattered)
+    operands, sc_in = [], []
+    for part in scattered:
+        left, right = part if isinstance(part, tuple) else (part, None)
+        blocks = left.reshape(owners, left.shape[0] // owners, left.shape[1])
+        operands += [blocks] if right is None else [blocks, right]
+        width = left.shape[1] if right is None else right.shape[1]
+        sc_in.append(jax.ShapeDtypeStruct(blocks.shape[:2] + (width,), f32))
     pieces = []
     for part in sc_in:
         count = 4
@@ -479,25 +496,26 @@
     scratch += [pltpu.SemaphoreType.DMA((2, n_ctx - 1, n_dp, count)) for count in pieces]
     scratch += [pltpu.VMEM((2, n_dp) + part.shape[1:], f32) for part in sc_in]
     scratch += [pltpu.SemaphoreType.DMA((2, 2, n_dp, count)) for count in pieces]
+    scratch += [pltpu.VMEM(part.shape, f32) for part, is_made in zip(sc_in, made) if is_made]
     if tail:
         scratch += [
             pltpu.VMEM((n_ten, tail, scattered[-1].shape[1]), f32),
             pltpu.SemaphoreType.DMA((2, n_ten - 1)),
         ]
     outs = pl.pallas_call(
-        functools.partial(sums_kernel, (n_ctx, n_dp, n_ten), len(whole), tuple(pieces), tail),
+        functools.partial(sums_kernel, (n_ctx, n_dp, n_ten), len(whole), tuple(pieces), made, tail),
         out_shape=tuple(
             [jax.ShapeDtypeStruct(part.shape, f32) for part in whole_in]
             + [jax.ShapeDtypeStruct(part.shape[1:], f32) for part in sc_in]
         ),
-        in_specs=[pl.BlockSpec(memory_space=VMEM)] * (len(whole) + len(scattered)),
+        in_specs=[pl.BlockSpec(memory_space=VMEM)] * (len(whole) + len(operands)),
         out_specs=tuple([pl.BlockSpec(memory_space=VMEM)] * (len(whole) + len(scattered))),
         scratch_shapes=scratch,
         compiler_params=pltpu.CompilerParams(
             collective_id=collective_id, has_side_effects=True, vmem_limit_bytes=VMEM_LIMIT
         ),
         name=name,
-    )(*whole_in, *sc_in)
+    )(*whole_in, *operands)
     totals = [out.reshape(part.shape) for out, part in zip(outs, whole)]
     return totals, list(outs[len(whole) :])
 
@@ -610,23 +628,20 @@
     ffn_down_part = jnp.dot(mixed_act, w_ffn_down, preferred_element_type=f32)
     grad_out = cotangent.reshape(-1, model_width)
     grad_res = grad_out.astype(f32)
-    grad_down_t = jnp.einsum("rd,rf->df", grad_out, mixed_act, preferred_element_type=f32)
     grad_mixed = jnp.einsum("rd,fd->rf", grad_out, w_ffn_down, preferred_element_type=f32)
     grad_gate = (grad_mixed * ffn_up * silu_grad(ffn_gate)).astype(bf16)
     grad_up = (grad_mixed * jax.nn.silu(ffn_gate)).astype(bf16)
     grad_pair = jnp.concatenate([grad_gate, grad_up], axis=1)
-    grad_pair_w = jnp.einsum("rd,rf->df", normed_two, grad_pair, preferred_element_type=f32)
     ffn_part = jnp.einsum(
         "rf,df->rd", grad_gate, w_ffn_gate, preferred_element_type=f32
     ) + jnp.einsum("rf,df->rd", grad_up, w_ffn_up, preferred_element_type=f32)
     (grad_normed_two, ffn_sum), (pair_rows, down_rows) = summed_arrays(
-        [ffn_part, ffn_down_part], [grad_pair_w, grad_down_t], 0, 2, "sum_ffn"
+        [ffn_part, ffn_down_part], [(normed_two.T, grad_pair), (grad_out.T, mixed_act)], 0, 2, "sum_ffn"
     )
     result = (hidden_res + ffn_sum).astype(bf16).reshape(inputs.shape)
     grad_two_rows, grad_gain_two = norm_back(hidden_res, scale_two, norm_gain2, grad_normed_two)
     grad_hidden = grad_res + grad_two_rows
     grad_attn = grad_hidden.astype(bf16)
-    grad_out_t = jnp.einsum("rd,rv->dv", grad_attn, gated_bf, preferred_element_type=f32)
     grad_gated = jnp.einsum("rd,vd->rv", grad_attn, w_output, preferred_element_type=f32).reshape(
         -1, heads_here, value_dim
     )
@@ -675,7 +690,6 @@
     grad_v = grad_v_all.astype(bf16)
     grad_g = grad_gate_heads.reshape(-1, heads_here * value_dim).astype(bf16)
     grad_proj = jnp.concatenate([grad_q, grad_k, grad_v, grad_g], axis=1)
-    grad_proj_w = jnp.einsum("rd,rk->dk", normed_one, grad_proj, preferred_element_type=f32)
     attn_part = (
         jnp.einsum("rk,dk->rd", grad_q, w_query, preferred_element_type=f32)
         + jnp.einsum("rk,dk->rd", grad_k, w_key, preferred_element_type=f32)
@@ -711,7 +725,11 @@
     pack = jnp.concatenate([tensor_pack, local_pack], axis=1)
     tail = tensor_pack.shape[1]
     (grad_normed_one,), (proj_rows, out_rows, pack_rows) = summed_arrays(
-        [attn_part], [grad_proj_w, grad_out_t, pack.reshape(-1, 128)], tail, 4, "sum_attn_back"
+        [attn_part],
+        [(normed_one.T, grad_proj), (grad_attn.T, gated_bf), pack.reshape(-1, 128)],
+        tail,
+        4,
+        "sum_attn_back",
     )
     grad_one_rows, _ = norm_back(rows_in, scale_one, norm_gain1, grad_normed_one)
     grad_inputs = (grad_hidden + grad_one_rows).reshape(inputs.shape)

time: 346 us -> 333 us (0.962)
  matrix products: 39.6 us -> 27.7 us
    dot_general x4 -> x0, matrix products: 12.6 us -> none  [the longest x1 4.75 us: shards(): jnp.einsum('rd,rf->df', normed_two, grad_pair, preferred_element_type=f32)]
    dot_general x4 -> x0, local copies, waits for them, and re-layouts: 9.7 us -> none  [the longest x1 3.57 us: shards(): jnp.einsum('rd,rf->df', grad_out, mixed_act, preferred_element_type=f32)]
    transpose x0 -> x4, local copies, waits for them, and re-layouts: none -> 7.17 us  [the longest x2 4.08 us: shards(): (grad_normed_one,), (proj_rows, out_rows, pack_rows) = summed_arrays([att...]
    pallas_call x3, Pallas kernels: 219 us -> 216 us  [summed_arrays(): pl.pallas_call(functools.partial(sums_kernel, (n_ctx, n_dp, n_ten), len(w...]
    unnamed x121 -> x123, local copies, waits for them, and re-layouts: 12.4 us -> 13.9 us
where the time goes in v2:
time: 333 us; the launch traced here: 331 us
  Pallas kernels  232 us (70%)
  local copies, waits for them, and re-layouts  44.7 us (13%)
  matrix products  27.7 us (8%)
  other arithmetic  24.9 us (7%)
    pallas_call x3, Pallas kernels, summed_arrays(): pl.pallas_call(functools.partial(sums_kernel, (n_ctx, n_dp, n_ten), len(w...  216 us
    unnamed x123, local copies, waits for them, and re-layouts  13.9 us

profile of v2, /device:TPU:16, one launch (start us, length us, event | category | flops | bytes accessed | tf_op | source)
XLA Modules:
  0.0 330.8 jit_solution(12274796818628560703)
XLA Ops:
  8.7 2.9 fusion.20
  11.6 4.1 %gla_forward.1 = (f32[256,256]{1,0:T(8,128)}, f32[256,128]{1,0:T(8,128)}, f32[4,128,256]{2,1,0:T(8,128)}, f32[128,384]{1,0:T(8,128)}) custom-call(f32[256,128]{1,0:T(8,128)} %convolution_multiply_fusion.q_ref, f32[256,128]{1,0:T(8,128)} %fusion.43.k_ref, f32[256,256]{1,0:T(8,128)} %fusion.41.v_ref, f32[256,128]{1,0:T(8,128)} %get-tuple-element.104.r_ref), custom_call_target="tpu_custom_call" | custom-call | tf_op jit(solution)/shard_map/gla_forward/pallas_call | solution.py:73
  17.1 3.0 exchange.1.entry_ref
  24.8 31.0 %sum_attn.1 = f32[4,64,1024]{2,1,0:T(8,128)} custom-call(f32[4,64,1024]{2,1,0:T(8,128)} %fusion.22.refs_0_), custom_call_target="tpu_custom_call" | custom-call | tf_op jit(solution)/shard_map/sum_attn/pallas_call | solution.py:505
  55.8 2.4 multiply_reduce_fusion.3
  59.3 2.1 copy.58
  61.4 2.2 fusion.50
  70.1 100.4 %sum_ffn.1 = (f32[4,64,1024]{2,1,0:T(8,128)}, f32[4,64,1024]{2,1,0:T(8,128)}, f32[128,1408]{1,0:T(8,128)}, f32[128,704]{1,0:T(8,128)}) custom-call(f32[4,64,1024]{2,1,0:T(8,128)} %bitcast.172, f32[4,64,1024]{2,1,0:T(8,128)} %bitcast.173, bf16[8,128,256]{2,1,0:T(8,128)(2,1)} %bitcast.178, bf16[256,1408]{1,0:T(8,128)(2,1)} %pad_maximum_fusion.refs_3_, ...), custom_call_target="tpu_custom_call" | custom-call | tf_op jit(solution)/shard_map/sum_ffn/pallas_call | solution.py:505
  170.4 2.4 multiply_reduce_fusion.1
  174.2 1.9 copy.70
  176.1 1.7 fusion.6
  180.6 3.4 %exchange_back.1.later_ref = f32[128,256]{1,0:T(8,128)} custom-call(f32[128,384]{1,0:T(8,128)} %pad_maximum_fusion.2.pair_ref), custom_call_target="tpu_custom_call" | custom-call | tf_op jit(solution)/shard_map/exchange_back/pallas_call | solution.py:192
  183.9 5.9 %gla_backward.1 = (f32[256,128]{1,0:T(8,128)}, f32[256,128]{1,0:T(8,128)}, f32[256,256]{1,0:T(8,128)}, f32[256,128]{1,0:T(8,128)}) custom-call(f32[256,128]{1,0:T(8,128)} %convolution_multiply_fusion.q_ref, f32[256,128]{1,0:T(8,128)} %fusion.43.k_ref, f32[256,256]{1,0:T(8,128)} %fusion.41.v_ref, f32[256,128]{1,0:T(8,128)} %get-tuple-element.104.r_ref, ...), custom_call_target="tpu_custom_call" | custom-call | tf_op jit(solution)/shard_map/gla_backward/pallas_call | solution.py:140
  203.7 1.7 pad_maximum_fusion.1.refs_2_
  207.0 1.9 reshape.397
  208.9 2.0 copy.63
  211.0 2.1 fusion.47
  213.1 1.9 copy.69
  215.0 1.9 copy.68
  224.7 2.0 copy.62
  226.8 84.3 %sum_attn_back.1 = (f32[4,64,1024]{2,1,0:T(8,128)}, f32[128,768]{1,0:T(8,128)}, f32[128,256]{1,0:T(8,128)}, f32[32,128]{1,0:T(8,128)}) custom-call(f32[4,64,1024]{2,1,0:T(8,128)} %bitcast.167, bf16[8,128,256]{2,1,0:T(8,128)(2,1)} %bitcast.176, bf16[256,768]{1,0:T(8,128)(2,1)} %pad_maximum_fusion.1.refs_2_, bf16[8,128,256]{2,1,0:T(8,128)(2,1)} %bitcast.175, ...), custom_call_target="tpu_custom_call" | custom-call | tf_op jit(solution)/shard_map/sum_attn_back/pallas_call | solution.py:505
  311.2 1.7 copy.67
  318.6 3.7 %fusion.2 = (f32[1,256,1024]{2,1,0:T(8,128)}, bf16[1,256,1024]{2,1,0:T(8,128)(2,1)}) fusion(bf16[1,256,1024]{2,1,0:T(8,128)(2,1)S(1)} %copy-done.1, bf16[1,256,1024]{2,1,0:T(8,128)(2,1)S(1)} %copy-done.4, f32[256]{0:T(256)} %div.62, f32[1024]{0:T(1024)S(1)} %copy-done.38, f32[256]{0:T(256)S(1)} %copy-done.45, f32[256]{0:T(256)} %copy-done.51, ...), kind=kLoop, calls=%fused_computation.11 | loop fusion | flops 4980736 | bytes 6828032 | tf_op jit(solution)/shard_map/add | solution.py:735
  329.1 1.7 fusion.48
  (180 shorter events, 61.1 us)
Async XLA Ops:
  0.6 63.0 %copy-start = (bf16[1024,704]{0,1:T(8,128)(2,1)S(1)}, bf16[1024,704]{0,1:T(8,128)(2,1)}, u32[]{:S(2)}) copy-start(bf16[1024,704]{0,1:T(8,128)(2,1)} %param.29) | copy-start | bytes 4325380
  0.7 2.8 copy-start.1
  0.7 2.8 copy-start.35
  0.7 2.8 copy-start.27
  0.7 3.9 %copy-start.32 = (bf16[1024,128]{1,0:T(8,128)(2,1)S(1)}, bf16[1024,128]{1,0:T(8,128)(2,1)}, u32[]{:S(2)}) copy-start(bf16[1024,128]{1,0:T(8,128)(2,1)} %param.18) | copy-start | bytes 786436
  2.1 19.6 %copy-start.42 = (f32[256]{0:T(256)}, f32[256]{0:T(256)S(1)}, u32[]{:S(2)}) copy-start(f32[256]{0:T(256)S(1)} %add_rsqrt_fusion.1) | copy-start | bytes 3076
  3.5 3.1 copy-start.46
  4.6 3.1 copy-start.4
  11.5 10.2 %copy-start.22 = (bf16[1024,256]{1,0:T(8,128)(2,1)S(1)}, bf16[1024,256]{1,0:T(8,128)(2,1)}, u32[]{:S(2)}) copy-start(bf16[1024,256]{1,0:T(8,128)(2,1)} %param.21) | copy-start | bytes 1572868
  11.5 10.2 %copy-start.55 = (f32[256]{0:T(256)S(1)}, f32[256]{0:T(256)}, u32[]{:S(2)}) copy-start(f32[256]{0:T(256)} %param.25) | copy-start | bytes 3076
  55.8 2.5 copy-start.2
  58.4 117.8 %copy-start.49 = (f32[256]{0:T(256)}, f32[256]{0:T(256)S(1)}, u32[]{:S(2)}) copy-start(f32[256]{0:T(256)S(1)} %rsqrt.34) | copy-start | bytes 3076
  64.5 4.0 %copy-start.10 = (bf16[256,704]{1,0:T(8,128)(2,1)}, bf16[256,704]{1,0:T(8,128)(2,1)S(1)}, u32[]{:S(2)}) copy-start(bf16[256,704]{1,0:T(8,128)(2,1)S(1)} %get-tuple-element.90.refs_5_) | copy-start | bytes 1081348
  174.2 3.7 %copy-start.51 = (f32[256]{0:T(256)}, f32[256]{0:T(256)S(1)}, u32[]{:S(2)}) copy-start(f32[256]{0:T(256)S(1)} %div.56) | copy-start | bytes 3076
  179.2 4.7 %copy-start.8 = (f32[256,256]{1,0:T(8,128)}, f32[256,256]{1,0:T(8,128)S(1)}, u32[]{:S(2)}) copy-start(f32[256,256]{1,0:T(8,128)S(1)} %add_add_fusion.g_ref) | copy-start | bytes 786436
  179.2 10.6 %copy-start.33 = (f32[256,128]{1,0:T(8,128)S(1)}, f32[256,128]{1,0:T(8,128)}, u32[]{:S(2)}) copy-start(f32[256,128]{1,0:T(8,128)} %get-tuple-element.105) | copy-start | bytes 393220
  179.9 12.3 %copy-start.47 = (f32[256,16]{0,1:T(8,128)S(1)}, f32[256,16]{0,1:T(8,128)}, u32[]{:S(2)}) copy-start(f32[256,16]{0,1:T(8,128)} %copy-done.46) | copy-start | bytes 49156
  199.8 5.6 %copy-start.36 = (f32[1024]{0:T(1024)S(1)}, f32[1024]{0:T(1024)}, u32[]{:S(2)}) copy-start(f32[1024]{0:T(1024)} %param.17) | copy-start | bytes 12292
  199.8 5.6 %copy-start.43 = (f32[256]{0:T(256)S(1)}, f32[256]{0:T(256)}, u32[]{:S(2)}) copy-start(f32[256]{0:T(256)} %copy-done.42) | copy-start | bytes 3076
  202.1 3.4 %copy-start.17 = (bf16[256,128]{1,0:T(8,128)(2,1)}, bf16[256,128]{1,0:T(8,128)(2,1)S(1)}, u32[]{:S(2)}) copy-start(bf16[256,128]{1,0:T(8,128)(2,1)S(1)} %convert_element_type.89) | copy-start | bytes 196612
  226.8 88.5 %copy-start.38 = (f32[1024]{0:T(1024)S(1)}, f32[1024]{0:T(1024)}, u32[]{:S(2)}) copy-start(f32[1024]{0:T(1024)} %param.17) | copy-start | bytes 12292
  311.1 7.5 %copy-start.40 = (f32[1024]{0:T(1024)S(1)}, f32[1024]{0:T(1024)}, u32[]{:S(2)}) copy-start(f32[1024]{0:T(1024)} %param.27) | copy-start | bytes 12292
  311.1 7.5 %copy-start.45 = (f32[256]{0:T(256)S(1)}, f32[256]{0:T(256)}, u32[]{:S(2)}) copy-start(f32[256]{0:T(256)} %copy-done.42) | copy-start | bytes 3076
  311.2 7.5 %copy-start.50 = (f32[256]{0:T(256)S(1)}, f32[256]{0:T(256)}, u32[]{:S(2)}) copy-start(f32[256]{0:T(256)} %copy-done.49) | copy-start | bytes 3076
  (34 other events, 52.0 us)
